TPU v7x, 128 devices: a whole 4x4x4 slice. The times are simulated.
128 devices in a mesh: tm: 16 (over y, x), rows: 8 (over z, core).
Axes of the slice: x: 4, y: 4, z: 4, core: 2. Of those that a mesh axis runs over, the one named last changes fastest.
Arguments:
- observations: float32 [128, 1024], P('tm'), may hold values from -6 to 6
- observed: int32 [128], P('tm'), may hold values 0 or 1
- start_mean: float32 [1024], replicated, may hold values from -6 to 6
- transition: float32 [1024, 1024], P(('tm', 'rows')), may hold values from -1 to 1
- closed_loop: float32 [1024, 1024], P(('tm', 'rows')), may hold values from -1 to 1
- obs_gain: float32 [1024, 1024], replicated, may hold values from -0.0625 to 0.0625
- smooth_observed: float32 [1024, 1024], P(('tm', 'rows')), may hold values from -1 to 1
- smooth_missing: float32 [1024, 1024], P(('tm', 'rows')), may hold values from -1 to 1
Outputs:
- filtered: float32 [128, 1024], P('tm', 'rows')
- smoothed: float32 [128, 1024], P('tm', 'rows')
All inputs are finite; a program needn't handle non-finite values. No bound on the sum of `observed` on one device may be relied on, other than what follows from the above.
Results may differ from a plain program's by a relative error of at most 0.0003.
Values sent between devices are 32-bit elements; how exact they have to be, the bound alone decides.
No kernel may reach another device: no remote copies, remote signals or barrier semaphores. Data moves between devices by JAX's collectives and lax.ppermute only.
A program may use at most 128 MiB of HBM per device.

v0:
```python
from functools import partial

import jax
import jax.numpy as jnp
from jax import lax
from jax.experimental import pallas as pl
from jax.experimental.pallas import tpu as pltpu
from jax.sharding import PartitionSpec as P


ALL = ("tm", "rows")
SIDE = 4
CORES = 2
LANES = 128
SUB = 8
UNROLL = 128
VMEM_BYTES = 28 << 20


def device_id(y, x, z, c):
    return ((y % SIDE * SIDE + x % SIDE) * SIDE + z % SIDE) * CORES + c


def coords():
    return [(y, x, z, c) for y in range(SIDE) for x in range(SIDE) for z in range(SIDE) for c in range(CORES)]


def swap_cores(value):
    return lax.ppermute(value, ALL, [(device_id(y, x, z, c), device_id(y, x, z, 1 - c)) for y, x, z, c in coords()])


def along_z(value, k):
    return lax.ppermute(value, ALL, [(device_id(y, x, z, c), device_id(y, x, z + k, c)) for y, x, z, c in coords()])


def across(value, k, phase):
    pairs = []
    for y, x, z, c in coords():
        dx = k if (c == 0) == (phase == 0) else 0
        dy = k - dx
        pairs.append((device_id(y, x, z, c), device_id(y + dy, x + dx, z, c)))
    return lax.ppermute(value, ALL, pairs)


def tiles(rows):
    r, width = rows.shape
    n = width // LANES
    return rows.reshape(r // SUB, SUB, n, LANES).transpose(0, 2, 1, 3).reshape(r // SUB * n, SUB, LANES)


def whereabouts():
    tm = lax.axis_index("tm")
    rows = lax.axis_index("rows")
    return tm // SIDE, tm % SIDE, rows // CORES, rows % CORES


def load_matrices(place, own, par, mats, blocks):
    y, x, z, c = place

    def move(i, carry):
        k2 = i // SIDE
        kz = i % SIDE
        pz = (z - kz + SIDE) % SIDE
        for k3 in range(SIDE):
            for mine in (True, False):
                q = c if mine else 1 - c
                dy = jnp.where(q == 0, k3, k2)
                dx = jnp.where(q == 0, k2, k3)
                chip = ((y - dy + SIDE) % SIDE * SIDE + (x - dx + SIDE) % SIDE) * SIDE + pz
                src = (own if mine else par)[k3]
                mats[q, pl.ds(chip * blocks, blocks)] = src[k2, pl.ds(kz * blocks, blocks)]
        return carry

    lax.fori_loop(0, SIDE * SIDE, move, 0)


def load_inject(place, own, par, inject, first, count):
    y, x, _, c = place

    def move(k2, carry):
        for k3 in range(SIDE):
            for mine in (True, False):
                q = c if mine else 1 - c
                dy = jnp.where(q == 0, k3, k2)
                dx = jnp.where(q == 0, k2, k3)
                seg = (y - dy + SIDE) % SIDE * SIDE + (x - dx + SIDE) % SIDE
                src = (own if mine else par)[k3]
                inject[pl.ds(seg * 2 * count + q * count, count)] = src[k2, first : first + count]
        return carry

    lax.fori_loop(0, SIDE, move, 0)


def load_seen(place, own, seen, sem, first):
    y, x, _, c = place
    for k3 in range(SIDE):
        for k2 in range(SIDE):
            dy = jnp.where(c == 0, k3, k2)
            dx = jnp.where(c == 0, k2, k3)
            seg = (y - dy + SIDE) % SIDE * SIDE + (x - dx + SIDE) % SIDE
            pltpu.make_async_copy(own[k3].at[k2, first], seen.at[seg], sem).start()


def transpose_matrices(mats, mats_t, groups):
    def block(i, carry):
        s = i // (groups * groups)
        b = i // groups % groups
        k = i % groups
        rows = [mats[s, (b * 16 + r) * groups + k] for r in range(16)]
        flipped = jnp.concatenate(rows, 0).T
        for r in range(16):
            mats_t[s, (k * 16 + r) * groups + b] = flipped[r * SUB : (r + 1) * SUB]
        return carry

    lax.fori_loop(0, 2 * groups * groups, block, 0, unroll=16)


def run_chain(seen, mats, mats_t, inject, inject_t, start, out, out_t, reverse):
    steps, dim = out.shape
    groups = dim // LANES
    row_blocks = dim // SUB
    lane = lax.broadcasted_iota(jnp.int32, (SUB, LANES), 1)

    def pick(t):
        return (seen[t // SUB, t % SUB, 0] > 0.5).astype(jnp.int32)

    def pair(p, state):
        first = steps - 1 - 2 * p if reverse else 2 * p
        second = first - 1 if reverse else first + 1
        s0, s1 = pick(first), pick(second)
        here = lane == first

        def rows(j, sums):
            r = pl.multiple_of(j * SUB, SUB)
            a = mats[s0, pl.ds(j * groups, groups)]
            prods = [a[k] * state[k] for k in range(groups)]
            while len(prods) > 1:
                prods = [prods[i] + prods[i + 1] for i in range(0, len(prods), 2)]
            total = prods[0] + jnp.where(here, inject_t[pl.ds(r, SUB), :], 0.0)
            col = jnp.broadcast_to(jnp.sum(total, 1, keepdims=True), (SUB, LANES))
            pltpu.store(out_t.at[pl.ds(r, SUB), :], col, mask=here)
            b = mats_t[s1, pl.ds(j * groups, groups)]
            return tuple(sums[k] + b[k] * col for k in range(groups))

        zero = tuple(jnp.zeros((SUB, LANES), jnp.float32) for _ in range(groups))
        sums = lax.fori_loop(0, row_blocks, rows, zero, unroll=UNROLL)
        row = jnp.concatenate([jnp.sum(v, 0, keepdims=True) for v in sums], 1) + inject[pl.ds(second, 1), :]
        out[pl.ds(second, 1), :] = row
        return tuple(jnp.broadcast_to(row[:, k * LANES : (k + 1) * LANES], (SUB, LANES)) for k in range(groups))

    lax.fori_loop(0, steps // 2, pair, start)
    odd = lax.broadcasted_iota(jnp.int32, (steps, LANES), 0) % 2
    from_t = odd == (1 if reverse else 0)
    for k in range(groups):
        cols = slice(k * LANES, (k + 1) * LANES)
        out[:, cols] = jnp.where(from_t, out_t[cols, :].T, out[:, cols])


def split(value):
    high = value.astype(jnp.bfloat16)
    return high, (value - high.astype(jnp.float32)).astype(jnp.bfloat16)


def predict(states, mats_t, out, groups):
    high, low = split(states[...])
    dot = partial(jnp.dot, preferred_element_type=jnp.float32)
    width = 2
    for b in range(0, groups, width):
        weights = jnp.concatenate(
            [
                jnp.concatenate([mats_t[0, j * groups + b + i] for j in range(groups * 16)], 0)
                for i in range(width)
            ],
            1,
        )
        w_high, w_low = split(weights)
        out[:, b * LANES : (b + width) * LANES] = dot(high, w_high) + (dot(low, w_high) + dot(high, w_low))


def send_block(place, value, block, sem):
    y, x, z, c = place
    seg_steps, width = block.shape
    corner = pl.ds((y * SIDE + x) * seg_steps, seg_steps), pl.ds((z * CORES + c) * width, width)
    pltpu.make_async_copy(value.at[corner], block, sem).start()


def forward_kernel(start, *refs, groups):
    own, par = refs[:SIDE], refs[SIDE : 2 * SIDE]
    block, error, prior, filtered, seen, mats, mats_t, inject_tiles, inject, inject_t, out_t, sems = refs[2 * SIDE :]
    blocks = 2 * groups
    half = groups // 2
    place = whereabouts()
    load_seen(place, own, seen, sems.at[0], SIDE * blocks + half)
    load_matrices(place, own, par, mats, blocks)
    load_inject(place, own, par, inject_tiles, SIDE * blocks, half)
    for seg in range(inject_tiles.shape[0] // groups):
        for k in range(groups):
            inject[seg * SUB : (seg + 1) * SUB, k * LANES : (k + 1) * LANES] = inject_tiles[seg * groups + k]
    for k in range(groups):
        cols = slice(k * LANES, (k + 1) * LANES)
        inject_t[cols, :] = inject[:, cols].T
    transpose_matrices(mats, mats_t, groups)
    first = tuple(jnp.broadcast_to(start[:, k * LANES : (k + 1) * LANES], (SUB, LANES)) for k in range(groups))
    pltpu.make_async_copy(seen, seen, sems.at[0]).wait()
    run_chain(seen, mats, mats_t, inject, inject_t, first, filtered, out_t, False)
    send_block(place, filtered, block, sems.at[1])
    predict(filtered, mats_t, inject, groups)
    row = lax.broadcasted_iota(jnp.int32, (filtered.shape[0], LANES), 0)
    for k in range(groups):
        cols = slice(k * LANES, (k + 1) * LANES)
        shifted = jnp.where(row == 0, 0.0, pltpu.roll(inject[:, cols], 1, 0))
        prior[:, cols] = shifted
        error[:, cols] = filtered[:, cols] - shifted
    pltpu.make_async_copy(filtered.at[: block.shape[0], : block.shape[1]], block, sems.at[1]).wait()


def backward_kernel(error, prior, *refs, groups):
    own, par, fwd = refs[:SIDE], refs[SIDE : 2 * SIDE], refs[2 * SIDE : 3 * SIDE]
    block, smoothed, seen, mats, mats_t, inject_t, out_t, sems = refs[3 * SIDE :]
    blocks = 2 * groups
    place = whereabouts()
    load_seen(place, fwd, seen, sems.at[0], SIDE * blocks + groups // 2)
    load_matrices(place, own, par, mats, blocks)
    for k in range(groups):
        cols = slice(k * LANES, (k + 1) * LANES)
        inject_t[cols, :] = error[:, cols].T
    transpose_matrices(mats, mats_t, groups)
    first = tuple(jnp.zeros((SUB, LANES), jnp.float32) for _ in range(groups))
    pltpu.make_async_copy(seen, seen, sems.at[0]).wait()
    run_chain(seen, mats, mats_t, error, inject_t, first, smoothed, out_t, True)
    smoothed[...] += prior[...]
    send_block(place, smoothed, block, sems.at[1])
    pltpu.make_async_copy(smoothed.at[: block.shape[0], : block.shape[1]], block, sems.at[1]).wait()


def shards(observations, observed, start_mean, transition, closed_loop, obs_gain, smooth_observed, smooth_missing):
    seg_steps, dim = observations.shape
    groups = dim // LANES
    steps = seg_steps * lax.axis_size("tm")
    c = lax.axis_index("rows") % CORES
    is_zero = c == 0

    fwd_0, fwd_1 = tiles(transition), tiles(closed_loop)
    bwd_0, bwd_1 = tiles(smooth_missing), tiles(smooth_observed)
    set_0 = jnp.stack([fwd_0, bwd_0])
    set_1 = jnp.stack([fwd_1, bwd_1])
    mine = jnp.where(is_zero, set_0, set_1)
    other = swap_cores(jnp.where(is_zero, set_1, set_0))
    unit = jnp.where(is_zero, jnp.concatenate([mine, other], 1), jnp.concatenate([other, mine], 1))

    gain_rows = lax.dynamic_slice_in_dim(obs_gain, c * (dim // 2), dim // 2, 0)
    seen_float = observed.astype(jnp.float32)
    inject = (
        lax.dot_general(observations, gain_rows, (((1,), (1,)), ((), ())), precision=lax.Precision.HIGHEST)
        * seen_float[:, None]
    )
    level = [unit]
    for k in range(1, SIDE):
        level.append(along_z(unit, k))
    inject = lax.optimization_barrier(inject)
    seen_tile = jnp.broadcast_to(seen_float[:, None], (seg_steps, LANES))[None]
    packed = jnp.concatenate([u[0] for u in level] + [tiles(inject), seen_tile] + [u[1] for u in level], 0)
    cut = SIDE * 2 * groups + groups // 2 + 1

    packs = [packed] + [across(packed, k, 0) for k in range(1, SIDE)]
    fwd = jnp.stack([p[:cut] for p in packs])
    bwd = jnp.stack([p[cut:] for p in packs])
    fwd_own = [fwd] + [across(fwd, k, 1) for k in range(1, SIDE)]
    fwd_par = [swap_cores(v) for v in fwd_own]
    bwd_own = [bwd] + [across(bwd, k, 1) for k in range(1, SIDE)]
    vmem = pl.BlockSpec(memory_space=pltpu.VMEM)
    any_space = pl.BlockSpec(memory_space=pl.ANY)
    full = jax.ShapeDtypeStruct((steps, dim), jnp.float32)
    mats = pltpu.VMEM((2, dim // SUB * groups, SUB, LANES), jnp.float32)
    wide = pltpu.VMEM((steps, dim), jnp.float32)
    tall = pltpu.VMEM((dim, steps), jnp.float32)
    seen = pltpu.SMEM((steps // SUB, SUB, LANES), jnp.float32)
    out_block = jax.ShapeDtypeStruct((seg_steps, LANES), jnp.float32)
    filtered, error, prior = pl.pallas_call(
        partial(forward_kernel, groups=groups),
        out_shape=(out_block, full, full),
        in_specs=[vmem] * (1 + 2 * SIDE),
        out_specs=(any_space, vmem, vmem),
        scratch_shapes=[
            wide,
            seen,
            mats,
            mats,
            pltpu.VMEM((steps // SUB * groups, SUB, LANES), jnp.float32),
            wide,
            tall,
            tall,
            pltpu.SemaphoreType.DMA((2,)),
        ],
        compiler_params=pltpu.CompilerParams(vmem_limit_bytes=VMEM_BYTES),
        name="forward_chain",
    )(start_mean.reshape(1, dim), *fwd_own, *fwd_par)

    *moved, error = lax.optimization_barrier((*bwd_own[1:], error))
    bwd_own = bwd_own[:1] + moved
    bwd_par = [swap_cores(v) for v in bwd_own]
    smoothed = pl.pallas_call(
        partial(backward_kernel, groups=groups),
        out_shape=out_block,
        in_specs=[vmem] * (2 + 2 * SIDE) + [any_space] * SIDE,
        out_specs=any_space,
        scratch_shapes=[wide, seen, mats, mats, tall, tall, pltpu.SemaphoreType.DMA((2,))],
        compiler_params=pltpu.CompilerParams(vmem_limit_bytes=VMEM_BYTES),
        name="backward_chain",
    )(error, prior, *bwd_own, *bwd_par, *fwd_own)
    return filtered, smoothed


def solution(mesh):
    return jax.shard_map(
        shards,
        mesh=mesh,
        in_specs=(
            P("tm", None),
            P("tm"),
            P(),
            P(("tm", "rows"), None),
            P(("tm", "rows"), None),
            P(),
            P(("tm", "rows"), None),
            P(("tm", "rows"), None),
        ),
        out_specs=(P("tm", "rows"), P("tm", "rows")),
        check_vma=False,
    )
```

profile of v0, /device:TPU:1, one launch (start us, length us, event | category | flops | bytes accessed | tf_op | source)
XLA Modules:
  0.0 167.7 jit_solution(11398135859499856922)
XLA Ops:
  0.6 0.0 copy-start
  0.7 0.8 fusion.17
  1.5 1.5 collective-permute-start
  2.9 0.7 convert_element_type.3
  3.6 3.4 %fusion.5 = f32[8,512]{1,0:T(8,128)S(1)} fusion(f32[8,1024]{1,0:T(8,128)S(1)} %copy-done, f32[1024,1024]{1,0:T(8,128)} %param.13, s32[]{:T(128)S(6)} %select_n.36, f32[8]{0:T(128)S(1)} %convert_element_type.3), kind=kOutput, calls=%fused_computation.4 | convolution fusion | flops 50335744 | bytes 2146340 | tf_op jit(solution)/shard_map/dot_general | solution.py:254
  7.0 0.0 collective-permute-done
  7.1 1.8 %collective-permute-start.1 = (f32[2,16,8,128]{3,2,1,0:T(8,128)S(1)}, f32[2,16,8,128]{3,2,1,0:T(8,128)S(1)}, u32[]{:S(2)}, u32[]{:S(2)}) collective-permute-start(f32[2,16,8,128]{3,2,1,0:T(8,128)S(1)} %maximum_select_fusion), channel_id=1, source_target_pairs={{0,2},{1,3},{2,4},{3,5},{4,6},{5,7},{6,0},{7,1},{8,10},{9,11},{10,... | collective-permute-start | bytes 393224 | tf_op jit(solution)/shard_map/ppermute | solution.py:33
  8.9 3.3 %collective-permute-start.2 = (f32[2,16,8,128]{3,2,1,0:T(8,128)S(1)}, f32[2,16,8,128]{3,2,1,0:T(8,128)S(1)}, u32[]{:S(2)}, u32[]{:S(2)}) collective-permute-start(f32[2,16,8,128]{3,2,1,0:T(8,128)S(1)} %maximum_select_fusion), channel_id=1, source_target_pairs={{0,4},{1,5},{2,6},{3,7},{4,0},{5,1},{6,2},{7,3},{8,12},{9,13},{10,... | collective-permute-start | bytes 393224 | tf_op jit(solution)/shard_map/ppermute | solution.py:33
  12.2 0.7 collective-permute-start.3
  12.9 1.9 %collective-permute-done.1 = f32[2,16,8,128]{3,2,1,0:T(8,128)S(1)} collective-permute-done((f32[2,16,8,128]{3,2,1,0:T(8,128)S(1)}, f32[2,16,8,128]{3,2,1,0:T(8,128)S(1)}, u32[]{:S(2)}, u32[]{:S(2)}) %collective-permute-start.1) | collective-permute-done | bytes 131104 | tf_op jit(solution)/shard_map/ppermute | solution.py:33
  14.9 3.7 %collective-permute-done.2 = f32[2,16,8,128]{3,2,1,0:T(8,128)S(1)} collective-permute-done((f32[2,16,8,128]{3,2,1,0:T(8,128)S(1)}, f32[2,16,8,128]{3,2,1,0:T(8,128)S(1)}, u32[]{:S(2)}, u32[]{:S(2)}) %collective-permute-start.2) | collective-permute-done | bytes 131104 | tf_op jit(solution)/shard_map/ppermute | solution.py:33
  18.6 0.0 collective-permute-done.3
  18.6 0.1 constant_dynamic-update-slice_fusion.6
  18.8 2.8 %collective-permute-start.6 = (f32[133,8,128]{2,1,0:T(8,128)S(1)}, f32[133,8,128]{2,1,0:T(8,128)S(1)}, u32[]{:S(2)}, u32[]{:S(2)}) collective-permute-start(f32[133,8,128]{2,1,0:T(8,128)S(1)} %get-tuple-element.17), channel_id=1, source_target_pairs={{0,24},{1,97},{2,26},{3,99},{4,28},{5,101},{6,30},{7,103},{8,0},{9... | collective-permute-start | bytes 1634312 | tf_op jit(solution)/shard_map/ppermute | solution.py:42
  21.6 0.3 collective-permute-start.5
  21.9 0.7 collective-permute-start.4
  22.6 0.1 constant_dynamic-update-slice_fusion
  22.7 11.1 %collective-permute-done.6 = f32[133,8,128]{2,1,0:T(8,128)S(1)} collective-permute-done((f32[133,8,128]{2,1,0:T(8,128)S(1)}, f32[133,8,128]{2,1,0:T(8,128)S(1)}, u32[]{:S(2)}, u32[]{:S(2)}) %collective-permute-start.6) | collective-permute-done | bytes 544800 | tf_op jit(solution)/shard_map/ppermute | solution.py:42
  33.8 0.0 collective-permute-done.5
  33.8 3.6 %collective-permute-done.4 = f32[133,8,128]{2,1,0:T(8,128)S(1)} collective-permute-done((f32[133,8,128]{2,1,0:T(8,128)S(1)}, f32[133,8,128]{2,1,0:T(8,128)S(1)}, u32[]{:S(2)}, u32[]{:S(2)}) %collective-permute-start.4) | collective-permute-done | bytes 544800 | tf_op jit(solution)/shard_map/ppermute | solution.py:42
  37.5 0.1 pad_maximum_fusion.refs_0_.refs_8_
  37.5 1.0 collective-permute-start.7
  38.5 2.5 %collective-permute-start.8 = (f32[4,69,8,128]{3,2,1,0:T(8,128)S(1)}, f32[4,69,8,128]{3,2,1,0:T(8,128)S(1)}, u32[]{:S(2)}, u32[]{:S(2)}) collective-permute-start(f32[4,69,8,128]{3,2,1,0:T(8,128)S(1)} %pad_maximum_fusion.refs_0_.refs_8_), channel_id=1, source_target_pairs={{0,64},{1,17},{2,66},{3,19},{4,68},{5,21},{6,70},{7,23},{8,72},{9,... | collective-permute-start | bytes 3391496 | tf_op jit(solution)/shard_map/ppermute | solution.py:42
  41.1 1.2 collective-permute-start.9
  42.2 3.1 %collective-permute-start.10 = (f32[4,69,8,128]{3,2,1,0:T(8,128)S(1)}, f32[4,69,8,128]{3,2,1,0:T(8,128)S(1)}, u32[]{:S(2)}, u32[]{:S(2)}) collective-permute-start(f32[4,69,8,128]{3,2,1,0:T(8,128)S(1)} %pad_maximum_fusion.refs_0_.refs_8_), channel_id=1, source_target_pairs={{0,1},{1,0},{2,3},{3,2},{4,5},{5,4},{6,7},{7,6},{8,9},{9,8},{10,11... | collective-permute-start | bytes 3391496 | tf_op jit(solution)/shard_map/ppermute | solution.py:29
  45.3 8.3 %collective-permute-done.7.refs_1_.refs_9_ = f32[4,69,8,128]{3,2,1,0:T(8,128)S(1)} collective-permute-done((f32[4,69,8,128]{3,2,1,0:T(8,128)S(1)}, f32[4,69,8,128]{3,2,1,0:T(8,128)S(1)}, u32[]{:S(2)}, u32[]{:S(2)}) %collective-permute-start.7) | collective-permute-done | bytes 1130528 | tf_op jit(solution)/shard_map/ppermute | solution.py:42
  53.7 2.6 %collective-permute-start.11 = (f32[4,69,8,128]{3,2,1,0:T(8,128)S(1)}, f32[4,69,8,128]{3,2,1,0:T(8,128)S(1)}, u32[]{:S(2)}, u32[]{:S(2)}) collective-permute-start(f32[4,69,8,128]{3,2,1,0:T(8,128)S(1)} %collective-permute-done.7.refs_1_.refs_9_), channel_id=1, source_target_pairs={{0,1},{1,0},{2,3},{3,2},{4,5},{5,4},{6,7},{7,6},{8,9},{9,8},{10,11... | collective-permute-start | bytes 3391496 | tf_op jit(solution)/shard_map/ppermute | solution.py:29
  56.4 0.0 copy-start.1
  56.4 10.1 %collective-permute-done.8.refs_2_.refs_10_ = f32[4,69,8,128]{3,2,1,0:T(8,128)S(1)} collective-permute-done((f32[4,69,8,128]{3,2,1,0:T(8,128)S(1)}, f32[4,69,8,128]{3,2,1,0:T(8,128)S(1)}, u32[]{:S(2)}, u32[]{:S(2)}) %collective-permute-start.8) | collective-permute-done | bytes 1130528 | tf_op jit(solution)/shard_map/ppermute | solution.py:42
  66.5 3.2 %collective-permute-start.12 = (f32[4,69,8,128]{3,2,1,0:T(8,128)S(1)}, f32[4,69,8,128]{3,2,1,0:T(8,128)S(1)}, u32[]{:S(2)}, u32[]{:S(2)}) collective-permute-start(f32[4,69,8,128]{3,2,1,0:T(8,128)S(1)} %collective-permute-done.8.refs_2_.refs_10_), channel_id=1, source_target_pairs={{0,1},{1,0},{2,3},{3,2},{4,5},{5,4},{6,7},{7,6},{8,9},{9,8},{10,11... | collective-permute-start | bytes 3391496 | tf_op jit(solution)/shard_map/ppermute | solution.py:29
  69.6 0.0 collective-permute-start.13
  69.6 0.1 pad_maximum_fusion.1.refs_0_
  69.7 0.1 collective-permute-start.14
  69.8 0.0 collective-permute-done.10.refs_4_
  69.8 1.5 collective-permute-start.15
  71.3 0.0 collective-permute-done.11.refs_5_
  71.3 1.2 collective-permute-start.16
  72.5 2.8 %collective-permute-start.17 = (f32[4,64,8,128]{3,2,1,0:T(8,128)S(1)}, f32[4,64,8,128]{3,2,1,0:T(8,128)S(1)}, u32[]{:S(2)}, u32[]{:S(2)}) collective-permute-start(f32[4,64,8,128]{3,2,1,0:T(8,128)S(1)} %pad_maximum_fusion.1.refs_0_), channel_id=1, source_target_pairs={{0,1},{1,0},{2,3},{3,2},{4,5},{5,4},{6,7},{7,6},{8,9},{9,8},{10,11... | collective-permute-start | bytes 3145736 | tf_op jit(solution)/shard_map/ppermute | solution.py:29
  75.4 0.0 collective-permute-done.13.refs_7_
  75.4 43.7 %forward_chain.1 = (f32[8,128]{1,0:T(8,128)}, f32[128,1024]{1,0:T(8,128)S(1)}, f32[128,1024]{1,0:T(8,128)S(1)}) custom-call(f32[1,1024]{1,0:T(1,128)S(1)} %bitcast.78, f32[4,69,8,128]{3,2,1,0:T(8,128)S(1)} %pad_maximum_fusion.refs_0_.refs_8_, f32[4,69,8,128]{3,2,1,0:T(8,128)S(1)} %collective-permute-done.7.refs_1_.refs_9_, ...), custom_call_target="tpu_custom_call" | custom-call | tf_op jit(solution)/shard_map/forward_chain/pallas_call | solution.py:279
  119.0 0.0 collective-permute-done.14.refs_1_
  119.1 0.2 collective-permute-start.18
  119.2 0.4 collective-permute-start.19
  119.7 0.1 collective-permute-start.20
  119.8 2.1 %collective-permute-done.18.refs_5_ = f32[4,64,8,128]{3,2,1,0:T(8,128)S(1)} collective-permute-done((f32[4,64,8,128]{3,2,1,0:T(8,128)S(1)}, f32[4,64,8,128]{3,2,1,0:T(8,128)S(1)}, u32[]{:S(2)}, u32[]{:S(2)}) %collective-permute-start.18) | collective-permute-done | bytes 1048608 | tf_op jit(solution)/shard_map/ppermute | solution.py:29
  121.8 1.5 collective-permute-done.19.refs_6_
  123.3 1.5 collective-permute-done.20.refs_7_
  124.8 42.8 %backward_chain.1 = f32[8,128]{1,0:T(8,128)} custom-call(f32[128,1024]{1,0:T(8,128)S(1)} %get-tuple-element.11.error, f32[128,1024]{1,0:T(8,128)S(1)} %get-tuple-element.12.prior, f32[4,64,8,128]{3,2,1,0:T(8,128)S(1)} %pad_maximum_fusion.1.refs_0_, f32[4,64,8,128]{3,2,1,0:T(8,128)S(1)} %collective-permute-done.14.refs_1_, ...), custom_call_target="tpu_custom_call" | custom-call | tf_op jit(solution)/shard_map/backward_chain/pallas_call | solution.py:302
  (29 shorter events, 0.3 us)
Async XLA Ops:
  0.6 3.0 %copy-start = (f32[8,1024]{1,0:T(8,128)S(1)}, f32[8,1024]{1,0:T(8,128)}, u32[]{:S(2)}) copy-start(f32[8,1024]{1,0:T(8,128)} %param.8) | copy-start | bytes 98308
  1.5 5.6 %collective-permute-start = (f32[2,8,8,128]{3,2,1,0:T(8,128)S(1)}, f32[2,8,8,128]{3,2,1,0:T(8,128)S(1)}, u32[]{:S(2)}, u32[]{:S(2)}) collective-permute-start(f32[2,8,8,128]{3,2,1,0:T(8,128)S(1)} %get-tuple-element.25), channel_id=1, source_target_pairs={{0,1},{1,0},{2,3},{3,2},{4,5},{5,4},{6,7},{7,6},{8,9},{9,8},{10,11... | collective-permute-start | bytes 196616 | tf_op jit(solution)/shard_map/ppermute | solution.py:29
  7.1 7.8 %collective-permute-start.1 = (f32[2,16,8,128]{3,2,1,0:T(8,128)S(1)}, f32[2,16,8,128]{3,2,1,0:T(8,128)S(1)}, u32[]{:S(2)}, u32[]{:S(2)}) collective-permute-start(f32[2,16,8,128]{3,2,1,0:T(8,128)S(1)} %maximum_select_fusion), channel_id=1, source_target_pairs={{0,2},{1,3},{2,4},{3,5},{4,6},{5,7},{6,0},{7,1},{8,10},{9,11},{10,... | collective-permute-start | bytes 393224 | tf_op jit(solution)/shard_map/ppermute | solution.py:33
  8.9 9.7 %collective-permute-start.2 = (f32[2,16,8,128]{3,2,1,0:T(8,128)S(1)}, f32[2,16,8,128]{3,2,1,0:T(8,128)S(1)}, u32[]{:S(2)}, u32[]{:S(2)}) collective-permute-start(f32[2,16,8,128]{3,2,1,0:T(8,128)S(1)} %maximum_select_fusion), channel_id=1, source_target_pairs={{0,4},{1,5},{2,6},{3,7},{4,0},{5,1},{6,2},{7,3},{8,12},{9,13},{10,... | collective-permute-start | bytes 393224 | tf_op jit(solution)/shard_map/ppermute | solution.py:33
  12.2 6.4 %collective-permute-start.3 = (f32[2,16,8,128]{3,2,1,0:T(8,128)S(1)}, f32[2,16,8,128]{3,2,1,0:T(8,128)S(1)}, u32[]{:S(2)}, u32[]{:S(2)}) collective-permute-start(f32[2,16,8,128]{3,2,1,0:T(8,128)S(1)} %maximum_select_fusion), channel_id=1, source_target_pairs={{0,6},{1,7},{2,0},{3,1},{4,2},{5,3},{6,4},{7,5},{8,14},{9,15},{10,... | collective-permute-start | bytes 393224 | tf_op jit(solution)/shard_map/ppermute | solution.py:33
  18.8 15.0 %collective-permute-start.6 = (f32[133,8,128]{2,1,0:T(8,128)S(1)}, f32[133,8,128]{2,1,0:T(8,128)S(1)}, u32[]{:S(2)}, u32[]{:S(2)}) collective-permute-start(f32[133,8,128]{2,1,0:T(8,128)S(1)} %get-tuple-element.17), channel_id=1, source_target_pairs={{0,24},{1,97},{2,26},{3,99},{4,28},{5,101},{6,30},{7,103},{8,0},{9... | collective-permute-start | bytes 1634312 | tf_op jit(solution)/shard_map/ppermute | solution.py:42
  21.6 12.2 %collective-permute-start.5 = (f32[133,8,128]{2,1,0:T(8,128)S(1)}, f32[133,8,128]{2,1,0:T(8,128)S(1)}, u32[]{:S(2)}, u32[]{:S(2)}) collective-permute-start(f32[133,8,128]{2,1,0:T(8,128)S(1)} %get-tuple-element.17), channel_id=1, source_target_pairs={{0,16},{1,65},{2,18},{3,67},{4,20},{5,69},{6,22},{7,71},{8,24},{9,... | collective-permute-start | bytes 1634312 | tf_op jit(solution)/shard_map/ppermute | solution.py:42
  21.9 15.5 %collective-permute-start.4 = (f32[133,8,128]{2,1,0:T(8,128)S(1)}, f32[133,8,128]{2,1,0:T(8,128)S(1)}, u32[]{:S(2)}, u32[]{:S(2)}) collective-permute-start(f32[133,8,128]{2,1,0:T(8,128)S(1)} %get-tuple-element.17), channel_id=1, source_target_pairs={{0,8},{1,33},{2,10},{3,35},{4,12},{5,37},{6,14},{7,39},{8,16},{9,4... | collective-permute-start | bytes 1634312 | tf_op jit(solution)/shard_map/ppermute | solution.py:42
  37.5 16.1 %collective-permute-start.7 = (f32[4,69,8,128]{3,2,1,0:T(8,128)S(1)}, f32[4,69,8,128]{3,2,1,0:T(8,128)S(1)}, u32[]{:S(2)}, u32[]{:S(2)}) collective-permute-start(f32[4,69,8,128]{3,2,1,0:T(8,128)S(1)} %pad_maximum_fusion.refs_0_.refs_8_), channel_id=1, source_target_pairs={{0,32},{1,9},{2,34},{3,11},{4,36},{5,13},{6,38},{7,15},{8,40},{9,1... | collective-permute-start | bytes 3391496 | tf_op jit(solution)/shard_map/ppermute | solution.py:42
  38.5 27.9 %collective-permute-start.8 = (f32[4,69,8,128]{3,2,1,0:T(8,128)S(1)}, f32[4,69,8,128]{3,2,1,0:T(8,128)S(1)}, u32[]{:S(2)}, u32[]{:S(2)}) collective-permute-start(f32[4,69,8,128]{3,2,1,0:T(8,128)S(1)} %pad_maximum_fusion.refs_0_.refs_8_), channel_id=1, source_target_pairs={{0,64},{1,17},{2,66},{3,19},{4,68},{5,21},{6,70},{7,23},{8,72},{9,... | collective-permute-start | bytes 3391496 | tf_op jit(solution)/shard_map/ppermute | solution.py:42
  41.1 28.5 %collective-permute-start.9 = (f32[4,69,8,128]{3,2,1,0:T(8,128)S(1)}, f32[4,69,8,128]{3,2,1,0:T(8,128)S(1)}, u32[]{:S(2)}, u32[]{:S(2)}) collective-permute-start(f32[4,69,8,128]{3,2,1,0:T(8,128)S(1)} %pad_maximum_fusion.refs_0_.refs_8_), channel_id=1, source_target_pairs={{0,96},{1,25},{2,98},{3,27},{4,100},{5,29},{6,102},{7,31},{8,104},... | collective-permute-start | bytes 3391496 | tf_op jit(solution)/shard_map/ppermute | solution.py:42
  42.2 27.5 %collective-permute-start.10 = (f32[4,69,8,128]{3,2,1,0:T(8,128)S(1)}, f32[4,69,8,128]{3,2,1,0:T(8,128)S(1)}, u32[]{:S(2)}, u32[]{:S(2)}) collective-permute-start(f32[4,69,8,128]{3,2,1,0:T(8,128)S(1)} %pad_maximum_fusion.refs_0_.refs_8_), channel_id=1, source_target_pairs={{0,1},{1,0},{2,3},{3,2},{4,5},{5,4},{6,7},{7,6},{8,9},{9,8},{10,11... | collective-permute-start | bytes 3391496 | tf_op jit(solution)/shard_map/ppermute | solution.py:29
  53.7 17.6 %collective-permute-start.11 = (f32[4,69,8,128]{3,2,1,0:T(8,128)S(1)}, f32[4,69,8,128]{3,2,1,0:T(8,128)S(1)}, u32[]{:S(2)}, u32[]{:S(2)}) collective-permute-start(f32[4,69,8,128]{3,2,1,0:T(8,128)S(1)} %collective-permute-done.7.refs_1_.refs_9_), channel_id=1, source_target_pairs={{0,1},{1,0},{2,3},{3,2},{4,5},{5,4},{6,7},{7,6},{8,9},{9,8},{10,11... | collective-permute-start | bytes 3391496 | tf_op jit(solution)/shard_map/ppermute | solution.py:29
  56.4 19.0 %copy-start.1 = (f32[1024]{0:T(1024)S(1)}, f32[1024]{0:T(1024)}, u32[]{:S(2)}) copy-start(f32[1024]{0:T(1024)} %param.10) | copy-start | bytes 12292
  66.5 6.1 %collective-permute-start.12 = (f32[4,69,8,128]{3,2,1,0:T(8,128)S(1)}, f32[4,69,8,128]{3,2,1,0:T(8,128)S(1)}, u32[]{:S(2)}, u32[]{:S(2)}) collective-permute-start(f32[4,69,8,128]{3,2,1,0:T(8,128)S(1)} %collective-permute-done.8.refs_2_.refs_10_), channel_id=1, source_target_pairs={{0,1},{1,0},{2,3},{3,2},{4,5},{5,4},{6,7},{7,6},{8,9},{9,8},{10,11... | collective-permute-start | bytes 3391496 | tf_op jit(solution)/shard_map/ppermute | solution.py:29
  69.6 5.7 %collective-permute-start.13 = (f32[4,69,8,128]{3,2,1,0:T(8,128)S(1)}, f32[4,69,8,128]{3,2,1,0:T(8,128)S(1)}, u32[]{:S(2)}, u32[]{:S(2)}) collective-permute-start(f32[4,69,8,128]{3,2,1,0:T(8,128)S(1)} %collective-permute-done.9.refs_3_.refs_11_), channel_id=1, source_target_pairs={{0,1},{1,0},{2,3},{3,2},{4,5},{5,4},{6,7},{7,6},{8,9},{9,8},{10,11... | collective-permute-start | bytes 3391496 | tf_op jit(solution)/shard_map/ppermute | solution.py:29
  69.7 49.3 %collective-permute-start.14 = (f32[4,64,8,128]{3,2,1,0:T(8,128)S(1)}, f32[4,64,8,128]{3,2,1,0:T(8,128)S(1)}, u32[]{:S(2)}, u32[]{:S(2)}) collective-permute-start(f32[4,64,8,128]{3,2,1,0:T(8,128)S(1)} %pad_maximum_fusion.1.refs_0_), channel_id=1, source_target_pairs={{0,32},{1,9},{2,34},{3,11},{4,36},{5,13},{6,38},{7,15},{8,40},{9,1... | collective-permute-start | bytes 3145736 | tf_op jit(solution)/shard_map/ppermute | solution.py:42
  69.8 49.3 %collective-permute-start.15 = (f32[4,64,8,128]{3,2,1,0:T(8,128)S(1)}, f32[4,64,8,128]{3,2,1,0:T(8,128)S(1)}, u32[]{:S(2)}, u32[]{:S(2)}) collective-permute-start(f32[4,64,8,128]{3,2,1,0:T(8,128)S(1)} %pad_maximum_fusion.1.refs_0_), channel_id=1, source_target_pairs={{0,64},{1,17},{2,66},{3,19},{4,68},{5,21},{6,70},{7,23},{8,72},{9,... | collective-permute-start | bytes 3145736 | tf_op jit(solution)/shard_map/ppermute | solution.py:42
  71.3 47.8 %collective-permute-start.16 = (f32[4,64,8,128]{3,2,1,0:T(8,128)S(1)}, f32[4,64,8,128]{3,2,1,0:T(8,128)S(1)}, u32[]{:S(2)}, u32[]{:S(2)}) collective-permute-start(f32[4,64,8,128]{3,2,1,0:T(8,128)S(1)} %pad_maximum_fusion.1.refs_0_), channel_id=1, source_target_pairs={{0,96},{1,25},{2,98},{3,27},{4,100},{5,29},{6,102},{7,31},{8,104},... | collective-permute-start | bytes 3145736 | tf_op jit(solution)/shard_map/ppermute | solution.py:42
  72.5 47.2 %collective-permute-start.17 = (f32[4,64,8,128]{3,2,1,0:T(8,128)S(1)}, f32[4,64,8,128]{3,2,1,0:T(8,128)S(1)}, u32[]{:S(2)}, u32[]{:S(2)}) collective-permute-start(f32[4,64,8,128]{3,2,1,0:T(8,128)S(1)} %pad_maximum_fusion.1.refs_0_), channel_id=1, source_target_pairs={{0,1},{1,0},{2,3},{3,2},{4,5},{5,4},{6,7},{7,6},{8,9},{9,8},{10,11... | collective-permute-start | bytes 3145736 | tf_op jit(solution)/shard_map/ppermute | solution.py:29
  119.1 2.7 %collective-permute-start.18 = (f32[4,64,8,128]{3,2,1,0:T(8,128)S(1)}, f32[4,64,8,128]{3,2,1,0:T(8,128)S(1)}, u32[]{:S(2)}, u32[]{:S(2)}) collective-permute-start(f32[4,64,8,128]{3,2,1,0:T(8,128)S(1)} %collective-permute-done.14.refs_1_), channel_id=1, source_target_pairs={{0,1},{1,0},{2,3},{3,2},{4,5},{5,4},{6,7},{7,6},{8,9},{9,8},{10,11... | collective-permute-start | bytes 3145736 | tf_op jit(solution)/shard_map/ppermute | solution.py:29
  119.2 4.1 %collective-permute-start.19 = (f32[4,64,8,128]{3,2,1,0:T(8,128)S(1)}, f32[4,64,8,128]{3,2,1,0:T(8,128)S(1)}, u32[]{:S(2)}, u32[]{:S(2)}) collective-permute-start(f32[4,64,8,128]{3,2,1,0:T(8,128)S(1)} %collective-permute-done.15.refs_2_), channel_id=1, source_target_pairs={{0,1},{1,0},{2,3},{3,2},{4,5},{5,4},{6,7},{7,6},{8,9},{9,8},{10,11... | collective-permute-start | bytes 3145736 | tf_op jit(solution)/shard_map/ppermute | solution.py:29
  119.7 5.1 %collective-permute-start.20 = (f32[4,64,8,128]{3,2,1,0:T(8,128)S(1)}, f32[4,64,8,128]{3,2,1,0:T(8,128)S(1)}, u32[]{:S(2)}, u32[]{:S(2)}) collective-permute-start(f32[4,64,8,128]{3,2,1,0:T(8,128)S(1)} %collective-permute-done.16.refs_3_), channel_id=1, source_target_pairs={{0,1},{1,0},{2,3},{3,2},{4,5},{5,4},{6,7},{7,6},{8,9},{9,8},{10,11... | collective-permute-start | bytes 3145736 | tf_op jit(solution)/shard_map/ppermute | solution.py:29
where the time goes:
time: 168 us
  Pallas kernels  86.5 us (51%)
  waiting for transfers between devices  43.8 us (26%)
  starting transfers between devices  31 us (18%)
  matrix products  3.43 us (2%)
    pallas_call x1, Pallas kernels, shards(): pl.pallas_call(partial(forward_kernel, groups=groups), out_shape=(out_blo...  43.7 us
    pallas_call x1, Pallas kernels, shards(): pl.pallas_call(partial(backward_kernel, groups=groups), out_shape=out_blo...  42.8 us
    ppermute x9, waiting for transfers between devices, across(): return lax.ppermute(value, ALL, pairs)  33.1 us
    ppermute x9, starting transfers between devices, swap_cores(): lax.ppermute(value, ALL, [(device_id(y, x, z, c), device_id(y, x, z, 1 -...  13.8 us
    ppermute x9, starting transfers between devices, across(): return lax.ppermute(value, ALL, pairs)  11.3 us
    ppermute x3, starting transfers between devices, along_z(): lax.ppermute(value, ALL, [(device_id(y, x, z, c), device_id(y, x, z + k,...  5.85 us
    ppermute x3, waiting for transfers between devices, along_z(): lax.ppermute(value, ALL, [(device_id(y, x, z, c), device_id(y, x, z + k,...  5.63 us
    ppermute x9, waiting for transfers between devices, swap_cores(): lax.ppermute(value, ALL, [(device_id(y, x, z, c), device_id(y, x, z, 1 -...  5.07 us
  transfers between devices with their start and end apart: 21, of which 9 were waited for; matrix products, arithmetic and copies ran while one was open for 3% of the time, Pallas kernels for 26%

commit v1 on v0

--- a/solution.py
+++ b/solution.py
@@ -14,7 +14,9 @@
 LANES = 128
 SUB = 8
 UNROLL = 128
+FIRST_STEPS = 80
 VMEM_BYTES = 28 << 20
+FIRST_BYTES = 8 << 20
 
 
 def device_id(y, x, z, c):
@@ -91,14 +93,17 @@
     lax.fori_loop(0, SIDE, move, 0)
 
 
-def load_seen(place, own, seen, sem, first):
+def load_seen(place, own, seen, first):
     y, x, _, c = place
+    lane = lax.broadcasted_iota(jnp.int32, (SUB, LANES), 1)
+    sub = lax.broadcasted_iota(jnp.int32, (SUB, LANES), 0)
     for k3 in range(SIDE):
         for k2 in range(SIDE):
             dy = jnp.where(c == 0, k3, k2)
             dx = jnp.where(c == 0, k2, k3)
             seg = (y - dy + SIDE) % SIDE * SIDE + (x - dx + SIDE) % SIDE
-            pltpu.make_async_copy(own[k3].at[k2, first], seen.at[seg], sem).start()
+            flags = jnp.where(lane == sub, own[k3][k2, first], 0.0)
+            seen[pl.ds(seg, 1), :] = jnp.sum(flags, 0, keepdims=True)
 
 
 def transpose_matrices(mats, mats_t, groups):
@@ -115,20 +120,21 @@
     lax.fori_loop(0, 2 * groups * groups, block, 0, unroll=16)
 
 
-def run_chain(seen, mats, mats_t, inject, inject_t, start, out, out_t, reverse):
-    steps, dim = out.shape
+def run_chain(seen, mats, mats_t, inject, inject_t, start, out, out_t, reverse, begin, count):
+    steps, dim = inject.shape
     groups = dim // LANES
     row_blocks = dim // SUB
     lane = lax.broadcasted_iota(jnp.int32, (SUB, LANES), 1)
 
     def pick(t):
-        return (seen[t // SUB, t % SUB, 0] > 0.5).astype(jnp.int32)
-
-    def pair(p, state):
-        first = steps - 1 - 2 * p if reverse else 2 * p
+        return (seen[t // SUB, t % SUB] > 0.5).astype(jnp.int32)
+
+    def pair(p, row):
+        first = steps - 1 - begin - 2 * p if reverse else begin + 2 * p
         second = first - 1 if reverse else first + 1
         s0, s1 = pick(first), pick(second)
         here = lane == first
+        state = [jnp.broadcast_to(row[:, k * LANES : (k + 1) * LANES], (SUB, LANES)) for k in range(groups)]
 
         def rows(j, sums):
             r = pl.multiple_of(j * SUB, SUB)
@@ -146,14 +152,16 @@
         sums = lax.fori_loop(0, row_blocks, rows, zero, unroll=UNROLL)
         row = jnp.concatenate([jnp.sum(v, 0, keepdims=True) for v in sums], 1) + inject[pl.ds(second, 1), :]
         out[pl.ds(second, 1), :] = row
-        return tuple(jnp.broadcast_to(row[:, k * LANES : (k + 1) * LANES], (SUB, LANES)) for k in range(groups))
-
-    lax.fori_loop(0, steps // 2, pair, start)
-    odd = lax.broadcasted_iota(jnp.int32, (steps, LANES), 0) % 2
+        return row
+
+    lax.fori_loop(0, count // 2, pair, start)
+    low = steps - begin - count if reverse else begin
+    odd = lax.broadcasted_iota(jnp.int32, (count, LANES), 0) % 2
     from_t = odd == (1 if reverse else 0)
     for k in range(groups):
         cols = slice(k * LANES, (k + 1) * LANES)
-        out[:, cols] = jnp.where(from_t, out_t[cols, :].T, out[:, cols])
+        flipped = out_t[cols, :].T[low : low + count]
+        out[low : low + count, cols] = jnp.where(from_t, flipped, out[low : low + count, cols])
 
 
 def split(value):
@@ -184,13 +192,15 @@
     pltpu.make_async_copy(value.at[corner], block, sem).start()
 
 
-def forward_kernel(start, *refs, groups):
+def first_kernel(start, *refs, groups):
     own, par = refs[:SIDE], refs[SIDE : 2 * SIDE]
-    block, error, prior, filtered, seen, mats, mats_t, inject_tiles, inject, inject_t, out_t, sems = refs[2 * SIDE :]
+    filtered, mats, mats_t, inject, inject_t, seen, inject_tiles, out_t, seen_now, sem = refs[2 * SIDE :]
     blocks = 2 * groups
     half = groups // 2
     place = whereabouts()
-    load_seen(place, own, seen, sems.at[0], SIDE * blocks + half)
+    load_seen(place, own, seen, SIDE * blocks + half)
+    copy_seen = pltpu.make_async_copy(seen, seen_now, sem.at[0])
+    copy_seen.start()
     load_matrices(place, own, par, mats, blocks)
     load_inject(place, own, par, inject_tiles, SIDE * blocks, half)
     for seg in range(inject_tiles.shape[0] // groups):
@@ -200,34 +210,49 @@
         cols = slice(k * LANES, (k + 1) * LANES)
         inject_t[cols, :] = inject[:, cols].T
     transpose_matrices(mats, mats_t, groups)
-    first = tuple(jnp.broadcast_to(start[:, k * LANES : (k + 1) * LANES], (SUB, LANES)) for k in range(groups))
-    pltpu.make_async_copy(seen, seen, sems.at[0]).wait()
-    run_chain(seen, mats, mats_t, inject, inject_t, first, filtered, out_t, False)
+    copy_seen.wait()
+    count = filtered.shape[0]
+    run_chain(seen_now, mats, mats_t, inject, inject_t, start[...], filtered, out_t, False, 0, count)
+
+
+def second_kernel(
+    seen, earlier, mats, mats_t, inject, inject_t, block, error, prior, filtered, predicted, out_t, seen_now, sems, *, groups
+):
+    place = whereabouts()
+    copy_seen = pltpu.make_async_copy(seen, seen_now, sems.at[0])
+    copy_seen.start()
+    done = earlier.shape[0]
+    filtered[:done, :] = earlier[...]
+    start = earlier[done - 1 : done, :]
+    copy_seen.wait()
+    count = filtered.shape[0] - done
+    run_chain(seen_now, mats, mats_t, inject, inject_t, start, filtered, out_t, False, done, count)
     send_block(place, filtered, block, sems.at[1])
-    predict(filtered, mats_t, inject, groups)
+    predict(filtered, mats_t, predicted, groups)
     row = lax.broadcasted_iota(jnp.int32, (filtered.shape[0], LANES), 0)
     for k in range(groups):
         cols = slice(k * LANES, (k + 1) * LANES)
-        shifted = jnp.where(row == 0, 0.0, pltpu.roll(inject[:, cols], 1, 0))
+        shifted = jnp.where(row == 0, 0.0, pltpu.roll(predicted[:, cols], 1, 0))
         prior[:, cols] = shifted
         error[:, cols] = filtered[:, cols] - shifted
     pltpu.make_async_copy(filtered.at[: block.shape[0], : block.shape[1]], block, sems.at[1]).wait()
 
 
-def backward_kernel(error, prior, *refs, groups):
-    own, par, fwd = refs[:SIDE], refs[SIDE : 2 * SIDE], refs[2 * SIDE : 3 * SIDE]
-    block, smoothed, seen, mats, mats_t, inject_t, out_t, sems = refs[3 * SIDE :]
+def backward_kernel(seen, error, prior, *refs, groups):
+    own, par = refs[:SIDE], refs[SIDE : 2 * SIDE]
+    block, smoothed, mats, mats_t, inject_t, out_t, seen_now, sems = refs[2 * SIDE :]
     blocks = 2 * groups
     place = whereabouts()
-    load_seen(place, fwd, seen, sems.at[0], SIDE * blocks + groups // 2)
+    copy_seen = pltpu.make_async_copy(seen, seen_now, sems.at[0])
+    copy_seen.start()
     load_matrices(place, own, par, mats, blocks)
     for k in range(groups):
         cols = slice(k * LANES, (k + 1) * LANES)
         inject_t[cols, :] = error[:, cols].T
     transpose_matrices(mats, mats_t, groups)
-    first = tuple(jnp.zeros((SUB, LANES), jnp.float32) for _ in range(groups))
-    pltpu.make_async_copy(seen, seen, sems.at[0]).wait()
-    run_chain(seen, mats, mats_t, error, inject_t, first, smoothed, out_t, True)
+    copy_seen.wait()
+    start = jnp.zeros((1, smoothed.shape[1]), jnp.float32)
+    run_chain(seen_now, mats, mats_t, error, inject_t, start, smoothed, out_t, True, 0, smoothed.shape[0])
     smoothed[...] += prior[...]
     send_block(place, smoothed, block, sems.at[1])
     pltpu.make_async_copy(smoothed.at[: block.shape[0], : block.shape[1]], block, sems.at[1]).wait()
@@ -270,44 +295,57 @@
     bwd_own = [bwd] + [across(bwd, k, 1) for k in range(1, SIDE)]
     vmem = pl.BlockSpec(memory_space=pltpu.VMEM)
     any_space = pl.BlockSpec(memory_space=pl.ANY)
-    full = jax.ShapeDtypeStruct((steps, dim), jnp.float32)
-    mats = pltpu.VMEM((2, dim // SUB * groups, SUB, LANES), jnp.float32)
+
+    def shape(*sizes):
+        return jax.ShapeDtypeStruct(sizes, jnp.float32)
+
+    segs = steps // SUB
+    first_steps = steps * FIRST_STEPS // LANES // SUB * SUB
+    mats_shape = (2, dim // SUB * groups, SUB, LANES)
+    mats = pltpu.VMEM(mats_shape, jnp.float32)
     wide = pltpu.VMEM((steps, dim), jnp.float32)
     tall = pltpu.VMEM((dim, steps), jnp.float32)
-    seen = pltpu.SMEM((steps // SUB, SUB, LANES), jnp.float32)
-    out_block = jax.ShapeDtypeStruct((seg_steps, LANES), jnp.float32)
-    filtered, error, prior = pl.pallas_call(
-        partial(forward_kernel, groups=groups),
-        out_shape=(out_block, full, full),
+    seen_now = pltpu.SMEM((segs, LANES), jnp.float32)
+    out_block = shape(seg_steps, LANES)
+    earlier, fwd_mats, fwd_mats_t, inject, inject_t, seen = pl.pallas_call(
+        partial(first_kernel, groups=groups),
+        out_shape=(
+            shape(first_steps, dim),
+            shape(*mats_shape),
+            shape(*mats_shape),
+            shape(steps, dim),
+            shape(dim, steps),
+            shape(segs, LANES),
+        ),
         in_specs=[vmem] * (1 + 2 * SIDE),
-        out_specs=(any_space, vmem, vmem),
-        scratch_shapes=[
-            wide,
-            seen,
-            mats,
-            mats,
-            pltpu.VMEM((steps // SUB * groups, SUB, LANES), jnp.float32),
-            wide,
-            tall,
-            tall,
-            pltpu.SemaphoreType.DMA((2,)),
-        ],
-        compiler_params=pltpu.CompilerParams(vmem_limit_bytes=VMEM_BYTES),
-        name="forward_chain",
+        out_specs=(vmem,) * 6,
+        scratch_shapes=[pltpu.VMEM((segs * groups, SUB, LANES), jnp.float32), tall, seen_now, pltpu.SemaphoreType.DMA((1,))],
+        compiler_params=pltpu.CompilerParams(vmem_limit_bytes=FIRST_BYTES),
+        name="forward_first",
     )(start_mean.reshape(1, dim), *fwd_own, *fwd_par)
 
-    *moved, error = lax.optimization_barrier((*bwd_own[1:], error))
+    *moved, earlier = lax.optimization_barrier((*bwd_own[1:], earlier))
     bwd_own = bwd_own[:1] + moved
     bwd_par = [swap_cores(v) for v in bwd_own]
+    filtered, error, prior = pl.pallas_call(
+        partial(second_kernel, groups=groups),
+        out_shape=(out_block, shape(steps, dim), shape(steps, dim)),
+        in_specs=[vmem] * 6,
+        out_specs=(any_space, vmem, vmem),
+        scratch_shapes=[wide, wide, tall, seen_now, pltpu.SemaphoreType.DMA((2,))],
+        compiler_params=pltpu.CompilerParams(vmem_limit_bytes=FIRST_BYTES),
+        name="forward_second",
+    )(seen, earlier, fwd_mats, fwd_mats_t, inject, inject_t)
+
     smoothed = pl.pallas_call(
         partial(backward_kernel, groups=groups),
         out_shape=out_block,
-        in_specs=[vmem] * (2 + 2 * SIDE) + [any_space] * SIDE,
+        in_specs=[vmem] * (3 + 2 * SIDE),
         out_specs=any_space,
-        scratch_shapes=[wide, seen, mats, mats, tall, tall, pltpu.SemaphoreType.DMA((2,))],
+        scratch_shapes=[wide, mats, mats, tall, tall, seen_now, pltpu.SemaphoreType.DMA((2,))],
         compiler_params=pltpu.CompilerParams(vmem_limit_bytes=VMEM_BYTES),
         name="backward_chain",
-    )(error, prior, *bwd_own, *bwd_par, *fwd_own)
+    )(seen, error, prior, *bwd_own, *bwd_par)
     return filtered, smoothed
 
 

time: 168 us -> 166 us (0.988)
  waiting for transfers between devices: 43.8 us -> 38.8 us
  Pallas kernels: 86.5 us -> 89.6 us
    ppermute x9, waiting for transfers between devices: 5.07 us -> 0.02 us  [swap_cores(): lax.ppermute(value, ALL, [(device_id(y, x, z, c), device_id(y, x, z, 1 -...]
    pallas_call x1 -> x2, Pallas kernels: 43.7 us -> 46.7 us  [the longest x1 30 us: shards(): pl.pallas_call(partial(first_kernel, groups=groups), out_shape=(shape(fir...]
  transfers between devices with their start and end apart: 21 -> 21, of which waited for: 9 -> 6; matrix products, arithmetic and copies ran while one was open for 3% -> 3% of each run, Pallas kernels for 26% -> 28%
where the time goes in v1:
time: 166 us
  Pallas kernels  89.6 us (54%)
  waiting for transfers between devices  38.8 us (23%)
  starting transfers between devices  31 us (19%)
  matrix products  3.43 us (2%)
  other arithmetic  1.67 us (1%)
    pallas_call x1, Pallas kernels, shards(): pl.pallas_call(partial(backward_kernel, groups=groups), out_shape=out_blo...  42.9 us
    ppermute x9, waiting for transfers between devices, across(): return lax.ppermute(value, ALL, pairs)  33.1 us
    pallas_call x1, Pallas kernels, shards(): pl.pallas_call(partial(first_kernel, groups=groups), out_shape=(shape(fir...  30 us
    pallas_call x1, Pallas kernels, shards(): pl.pallas_call(partial(second_kernel, groups=groups), out_shape=(out_bloc...  16.7 us
    ppermute x9, starting transfers between devices, swap_cores(): lax.ppermute(value, ALL, [(device_id(y, x, z, c), device_id(y, x, z, 1 -...  13.8 us
    ppermute x9, starting transfers between devices, across(): return lax.ppermute(value, ALL, pairs)  11.3 us
    ppermute x3, starting transfers between devices, along_z(): lax.ppermute(value, ALL, [(device_id(y, x, z, c), device_id(y, x, z + k,...  5.85 us
    ppermute x3, waiting for transfers between devices, along_z(): lax.ppermute(value, ALL, [(device_id(y, x, z, c), device_id(y, x, z + k,...  5.63 us
  transfers between devices with their start and end apart: 21, of which 6 were waited for; matrix products, arithmetic and copies ran while one was open for 3% of the time, Pallas kernels for 28%

profile of v1, /device:TPU:1, one launch (start us, length us, event | category | flops | bytes accessed | tf_op | source)
XLA Modules:
  0.0 165.9 jit_solution(2718639215519057292)
XLA Ops:
  0.6 0.0 copy-start
  0.7 0.8 fusion.17
  1.5 1.5 collective-permute-start
  2.9 0.7 convert_element_type.3
  3.6 3.4 %fusion.5 = f32[8,512]{1,0:T(8,128)S(1)} fusion(f32[8,1024]{1,0:T(8,128)S(1)} %copy-done, f32[1024,1024]{1,0:T(8,128)} %param.13, s32[]{:T(128)S(6)} %select_n.36, f32[8]{0:T(128)S(1)} %convert_element_type.3), kind=kOutput, calls=%fused_computation.4 | convolution fusion | flops 50335744 | bytes 2146340 | tf_op jit(solution)/shard_map/dot_general | solution.py:279
  7.0 0.0 collective-permute-done
  7.1 1.8 %collective-permute-start.1 = (f32[2,16,8,128]{3,2,1,0:T(8,128)S(1)}, f32[2,16,8,128]{3,2,1,0:T(8,128)S(1)}, u32[]{:S(2)}, u32[]{:S(2)}) collective-permute-start(f32[2,16,8,128]{3,2,1,0:T(8,128)S(1)} %maximum_select_fusion), channel_id=1, source_target_pairs={{0,2},{1,3},{2,4},{3,5},{4,6},{5,7},{6,0},{7,1},{8,10},{9,11},{10,... | collective-permute-start | bytes 393224 | tf_op jit(solution)/shard_map/ppermute | solution.py:35
  8.9 3.3 %collective-permute-start.2 = (f32[2,16,8,128]{3,2,1,0:T(8,128)S(1)}, f32[2,16,8,128]{3,2,1,0:T(8,128)S(1)}, u32[]{:S(2)}, u32[]{:S(2)}) collective-permute-start(f32[2,16,8,128]{3,2,1,0:T(8,128)S(1)} %maximum_select_fusion), channel_id=1, source_target_pairs={{0,4},{1,5},{2,6},{3,7},{4,0},{5,1},{6,2},{7,3},{8,12},{9,13},{10,... | collective-permute-start | bytes 393224 | tf_op jit(solution)/shard_map/ppermute | solution.py:35
  12.2 0.7 collective-permute-start.3
  12.9 1.9 %collective-permute-done.1 = f32[2,16,8,128]{3,2,1,0:T(8,128)S(1)} collective-permute-done((f32[2,16,8,128]{3,2,1,0:T(8,128)S(1)}, f32[2,16,8,128]{3,2,1,0:T(8,128)S(1)}, u32[]{:S(2)}, u32[]{:S(2)}) %collective-permute-start.1) | collective-permute-done | bytes 131104 | tf_op jit(solution)/shard_map/ppermute | solution.py:35
  14.9 3.7 %collective-permute-done.2 = f32[2,16,8,128]{3,2,1,0:T(8,128)S(1)} collective-permute-done((f32[2,16,8,128]{3,2,1,0:T(8,128)S(1)}, f32[2,16,8,128]{3,2,1,0:T(8,128)S(1)}, u32[]{:S(2)}, u32[]{:S(2)}) %collective-permute-start.2) | collective-permute-done | bytes 131104 | tf_op jit(solution)/shard_map/ppermute | solution.py:35
  18.6 0.0 collective-permute-done.3
  18.6 0.1 constant_dynamic-update-slice_fusion.6
  18.8 2.8 %collective-permute-start.6 = (f32[133,8,128]{2,1,0:T(8,128)S(1)}, f32[133,8,128]{2,1,0:T(8,128)S(1)}, u32[]{:S(2)}, u32[]{:S(2)}) collective-permute-start(f32[133,8,128]{2,1,0:T(8,128)S(1)} %get-tuple-element.29), channel_id=1, source_target_pairs={{0,24},{1,97},{2,26},{3,99},{4,28},{5,101},{6,30},{7,103},{8,0},{9... | collective-permute-start | bytes 1634312 | tf_op jit(solution)/shard_map/ppermute | solution.py:44
  21.6 0.3 collective-permute-start.5
  21.9 0.7 collective-permute-start.4
  22.6 0.1 constant_dynamic-update-slice_fusion
  22.7 11.1 %collective-permute-done.6 = f32[133,8,128]{2,1,0:T(8,128)S(1)} collective-permute-done((f32[133,8,128]{2,1,0:T(8,128)S(1)}, f32[133,8,128]{2,1,0:T(8,128)S(1)}, u32[]{:S(2)}, u32[]{:S(2)}) %collective-permute-start.6) | collective-permute-done | bytes 544800 | tf_op jit(solution)/shard_map/ppermute | solution.py:44
  33.8 0.0 collective-permute-done.5
  33.8 3.6 %collective-permute-done.4 = f32[133,8,128]{2,1,0:T(8,128)S(1)} collective-permute-done((f32[133,8,128]{2,1,0:T(8,128)S(1)}, f32[133,8,128]{2,1,0:T(8,128)S(1)}, u32[]{:S(2)}, u32[]{:S(2)}) %collective-permute-start.4) | collective-permute-done | bytes 544800 | tf_op jit(solution)/shard_map/ppermute | solution.py:44
  37.5 0.1 pad_maximum_fusion.refs_0_
  37.5 1.0 collective-permute-start.7
  38.5 2.5 %collective-permute-start.8 = (f32[4,69,8,128]{3,2,1,0:T(8,128)S(1)}, f32[4,69,8,128]{3,2,1,0:T(8,128)S(1)}, u32[]{:S(2)}, u32[]{:S(2)}) collective-permute-start(f32[4,69,8,128]{3,2,1,0:T(8,128)S(1)} %pad_maximum_fusion.refs_0_), channel_id=1, source_target_pairs={{0,64},{1,17},{2,66},{3,19},{4,68},{5,21},{6,70},{7,23},{8,72},{9,... | collective-permute-start | bytes 3391496 | tf_op jit(solution)/shard_map/ppermute | solution.py:44
  41.1 1.2 collective-permute-start.9
  42.2 3.1 %collective-permute-start.10 = (f32[4,69,8,128]{3,2,1,0:T(8,128)S(1)}, f32[4,69,8,128]{3,2,1,0:T(8,128)S(1)}, u32[]{:S(2)}, u32[]{:S(2)}) collective-permute-start(f32[4,69,8,128]{3,2,1,0:T(8,128)S(1)} %pad_maximum_fusion.refs_0_), channel_id=1, source_target_pairs={{0,1},{1,0},{2,3},{3,2},{4,5},{5,4},{6,7},{7,6},{8,9},{9,8},{10,11... | collective-permute-start | bytes 3391496 | tf_op jit(solution)/shard_map/ppermute | solution.py:31
  45.3 8.3 %collective-permute-done.7.refs_1_ = f32[4,69,8,128]{3,2,1,0:T(8,128)S(1)} collective-permute-done((f32[4,69,8,128]{3,2,1,0:T(8,128)S(1)}, f32[4,69,8,128]{3,2,1,0:T(8,128)S(1)}, u32[]{:S(2)}, u32[]{:S(2)}) %collective-permute-start.7) | collective-permute-done | bytes 1130528 | tf_op jit(solution)/shard_map/ppermute | solution.py:44
  53.7 2.6 %collective-permute-start.11 = (f32[4,69,8,128]{3,2,1,0:T(8,128)S(1)}, f32[4,69,8,128]{3,2,1,0:T(8,128)S(1)}, u32[]{:S(2)}, u32[]{:S(2)}) collective-permute-start(f32[4,69,8,128]{3,2,1,0:T(8,128)S(1)} %collective-permute-done.7.refs_1_), channel_id=1, source_target_pairs={{0,1},{1,0},{2,3},{3,2},{4,5},{5,4},{6,7},{7,6},{8,9},{9,8},{10,11... | collective-permute-start | bytes 3391496 | tf_op jit(solution)/shard_map/ppermute | solution.py:31
  56.4 0.0 copy-start.1
  56.4 10.1 %collective-permute-done.8.refs_2_ = f32[4,69,8,128]{3,2,1,0:T(8,128)S(1)} collective-permute-done((f32[4,69,8,128]{3,2,1,0:T(8,128)S(1)}, f32[4,69,8,128]{3,2,1,0:T(8,128)S(1)}, u32[]{:S(2)}, u32[]{:S(2)}) %collective-permute-start.8) | collective-permute-done | bytes 1130528 | tf_op jit(solution)/shard_map/ppermute | solution.py:44
  66.5 3.2 %collective-permute-start.12 = (f32[4,69,8,128]{3,2,1,0:T(8,128)S(1)}, f32[4,69,8,128]{3,2,1,0:T(8,128)S(1)}, u32[]{:S(2)}, u32[]{:S(2)}) collective-permute-start(f32[4,69,8,128]{3,2,1,0:T(8,128)S(1)} %collective-permute-done.8.refs_2_), channel_id=1, source_target_pairs={{0,1},{1,0},{2,3},{3,2},{4,5},{5,4},{6,7},{7,6},{8,9},{9,8},{10,11... | collective-permute-start | bytes 3391496 | tf_op jit(solution)/shard_map/ppermute | solution.py:31
  69.6 0.0 collective-permute-done.9.refs_3_
  69.6 0.0 collective-permute-start.13
  69.6 0.1 pad_maximum_fusion.1.refs_0_
  69.7 0.1 collective-permute-start.14
  69.8 1.5 collective-permute-start.15
  71.3 1.2 collective-permute-start.16
  72.5 2.8 %collective-permute-start.17 = (f32[4,64,8,128]{3,2,1,0:T(8,128)S(1)}, f32[4,64,8,128]{3,2,1,0:T(8,128)S(1)}, u32[]{:S(2)}, u32[]{:S(2)}) collective-permute-start(f32[4,64,8,128]{3,2,1,0:T(8,128)S(1)} %pad_maximum_fusion.1.refs_0_), channel_id=1, source_target_pairs={{0,1},{1,0},{2,3},{3,2},{4,5},{5,4},{6,7},{7,6},{8,9},{9,8},{10,11... | collective-permute-start | bytes 3145736 | tf_op jit(solution)/shard_map/ppermute | solution.py:31
  75.4 0.0 collective-permute-done.13.refs_7_
  75.4 30.0 %forward_first.1 = (f32[80,1024]{1,0:T(8,128)S(1)}, f32[2,1024,8,128]{3,2,1,0:T(8,128)S(1)}, f32[2,1024,8,128]{3,2,1,0:T(8,128)S(1)}, f32[128,1024]{1,0:T(8,128)...) custom-call(f32[1,1024]{1,0:T(1,128)S(1)} %bitcast.78, f32[4,69,8,128]{3,2,1,0:T(8,128)S(1)} %pad_maximum_fusion.refs_0_, ...), custom_call_target="tpu_custom_call" | custom-call | tf_op jit(solution)/shard_map/forward_first/pallas_call | solution.py:310
  105.4 0.0 collective-permute-done.15.refs_2_
  105.4 0.1 collective-permute-start.18
  105.5 0.5 collective-permute-start.19
  106.0 0.1 collective-permute-start.20
  106.1 16.7 %forward_second.1 = (f32[8,128]{1,0:T(8,128)}, f32[128,1024]{1,0:T(8,128)S(1)}, f32[128,1024]{1,0:T(8,128)S(1)}) custom-call(f32[16,128]{1,0:T(8,128)S(1)} %get-tuple-element.15.seen, f32[80,1024]{1,0:T(8,128)S(1)} %get-tuple-element.17.earlier, f32[2,1024,8,128]{3,2,1,0:T(8,128)S(1)} %get-tuple-element.18.mats, ...), custom_call_target="tpu_custom_call" | custom-call | tf_op jit(solution)/shard_map/forward_second/pallas_call | solution.py:330
  122.8 0.0 collective-permute-done.17.refs_4_
  122.8 0.0 collective-permute-done.19.refs_6_
  122.8 0.0 collective-permute-done.20.refs_7_
  122.8 42.9 %backward_chain.1 = f32[8,128]{1,0:T(8,128)} custom-call(f32[16,128]{1,0:T(8,128)S(1)} %get-tuple-element.15.seen, f32[128,1024]{1,0:T(8,128)S(1)} %get-tuple-element.23.error, f32[128,1024]{1,0:T(8,128)S(1)} %get-tuple-element.24.prior, f32[4,64,8,128]{3,2,1,0:T(8,128)S(1)} %pad_maximum_fusion.1.refs_0_, ...), custom_call_target="tpu_custom_call" | custom-call | tf_op jit(solution)/shard_map/backward_chain/pallas_call | solution.py:340
  (30 shorter events, 0.3 us)
Async XLA Ops:
  0.6 3.0 %copy-start = (f32[8,1024]{1,0:T(8,128)S(1)}, f32[8,1024]{1,0:T(8,128)}, u32[]{:S(2)}) copy-start(f32[8,1024]{1,0:T(8,128)} %param.8) | copy-start | bytes 98308
  1.5 5.6 %collective-permute-start = (f32[2,8,8,128]{3,2,1,0:T(8,128)S(1)}, f32[2,8,8,128]{3,2,1,0:T(8,128)S(1)}, u32[]{:S(2)}, u32[]{:S(2)}) collective-permute-start(f32[2,8,8,128]{3,2,1,0:T(8,128)S(1)} %get-tuple-element.37), channel_id=1, source_target_pairs={{0,1},{1,0},{2,3},{3,2},{4,5},{5,4},{6,7},{7,6},{8,9},{9,8},{10,11... | collective-permute-start | bytes 196616 | tf_op jit(solution)/shard_map/ppermute | solution.py:31
  7.1 7.8 %collective-permute-start.1 = (f32[2,16,8,128]{3,2,1,0:T(8,128)S(1)}, f32[2,16,8,128]{3,2,1,0:T(8,128)S(1)}, u32[]{:S(2)}, u32[]{:S(2)}) collective-permute-start(f32[2,16,8,128]{3,2,1,0:T(8,128)S(1)} %maximum_select_fusion), channel_id=1, source_target_pairs={{0,2},{1,3},{2,4},{3,5},{4,6},{5,7},{6,0},{7,1},{8,10},{9,11},{10,... | collective-permute-start | bytes 393224 | tf_op jit(solution)/shard_map/ppermute | solution.py:35
  8.9 9.7 %collective-permute-start.2 = (f32[2,16,8,128]{3,2,1,0:T(8,128)S(1)}, f32[2,16,8,128]{3,2,1,0:T(8,128)S(1)}, u32[]{:S(2)}, u32[]{:S(2)}) collective-permute-start(f32[2,16,8,128]{3,2,1,0:T(8,128)S(1)} %maximum_select_fusion), channel_id=1, source_target_pairs={{0,4},{1,5},{2,6},{3,7},{4,0},{5,1},{6,2},{7,3},{8,12},{9,13},{10,... | collective-permute-start | bytes 393224 | tf_op jit(solution)/shard_map/ppermute | solution.py:35
  12.2 6.4 %collective-permute-start.3 = (f32[2,16,8,128]{3,2,1,0:T(8,128)S(1)}, f32[2,16,8,128]{3,2,1,0:T(8,128)S(1)}, u32[]{:S(2)}, u32[]{:S(2)}) collective-permute-start(f32[2,16,8,128]{3,2,1,0:T(8,128)S(1)} %maximum_select_fusion), channel_id=1, source_target_pairs={{0,6},{1,7},{2,0},{3,1},{4,2},{5,3},{6,4},{7,5},{8,14},{9,15},{10,... | collective-permute-start | bytes 393224 | tf_op jit(solution)/shard_map/ppermute | solution.py:35
  18.8 15.0 %collective-permute-start.6 = (f32[133,8,128]{2,1,0:T(8,128)S(1)}, f32[133,8,128]{2,1,0:T(8,128)S(1)}, u32[]{:S(2)}, u32[]{:S(2)}) collective-permute-start(f32[133,8,128]{2,1,0:T(8,128)S(1)} %get-tuple-element.29), channel_id=1, source_target_pairs={{0,24},{1,97},{2,26},{3,99},{4,28},{5,101},{6,30},{7,103},{8,0},{9... | collective-permute-start | bytes 1634312 | tf_op jit(solution)/shard_map/ppermute | solution.py:44
  21.6 12.2 %collective-permute-start.5 = (f32[133,8,128]{2,1,0:T(8,128)S(1)}, f32[133,8,128]{2,1,0:T(8,128)S(1)}, u32[]{:S(2)}, u32[]{:S(2)}) collective-permute-start(f32[133,8,128]{2,1,0:T(8,128)S(1)} %get-tuple-element.29), channel_id=1, source_target_pairs={{0,16},{1,65},{2,18},{3,67},{4,20},{5,69},{6,22},{7,71},{8,24},{9,... | collective-permute-start | bytes 1634312 | tf_op jit(solution)/shard_map/ppermute | solution.py:44
  21.9 15.5 %collective-permute-start.4 = (f32[133,8,128]{2,1,0:T(8,128)S(1)}, f32[133,8,128]{2,1,0:T(8,128)S(1)}, u32[]{:S(2)}, u32[]{:S(2)}) collective-permute-start(f32[133,8,128]{2,1,0:T(8,128)S(1)} %get-tuple-element.29), channel_id=1, source_target_pairs={{0,8},{1,33},{2,10},{3,35},{4,12},{5,37},{6,14},{7,39},{8,16},{9,4... | collective-permute-start | bytes 1634312 | tf_op jit(solution)/shard_map/ppermute | solution.py:44
  37.5 16.1 %collective-permute-start.7 = (f32[4,69,8,128]{3,2,1,0:T(8,128)S(1)}, f32[4,69,8,128]{3,2,1,0:T(8,128)S(1)}, u32[]{:S(2)}, u32[]{:S(2)}) collective-permute-start(f32[4,69,8,128]{3,2,1,0:T(8,128)S(1)} %pad_maximum_fusion.refs_0_), channel_id=1, source_target_pairs={{0,32},{1,9},{2,34},{3,11},{4,36},{5,13},{6,38},{7,15},{8,40},{9,1... | collective-permute-start | bytes 3391496 | tf_op jit(solution)/shard_map/ppermute | solution.py:44
  38.5 27.9 %collective-permute-start.8 = (f32[4,69,8,128]{3,2,1,0:T(8,128)S(1)}, f32[4,69,8,128]{3,2,1,0:T(8,128)S(1)}, u32[]{:S(2)}, u32[]{:S(2)}) collective-permute-start(f32[4,69,8,128]{3,2,1,0:T(8,128)S(1)} %pad_maximum_fusion.refs_0_), channel_id=1, source_target_pairs={{0,64},{1,17},{2,66},{3,19},{4,68},{5,21},{6,70},{7,23},{8,72},{9,... | collective-permute-start | bytes 3391496 | tf_op jit(solution)/shard_map/ppermute | solution.py:44
  41.1 28.5 %collective-permute-start.9 = (f32[4,69,8,128]{3,2,1,0:T(8,128)S(1)}, f32[4,69,8,128]{3,2,1,0:T(8,128)S(1)}, u32[]{:S(2)}, u32[]{:S(2)}) collective-permute-start(f32[4,69,8,128]{3,2,1,0:T(8,128)S(1)} %pad_maximum_fusion.refs_0_), channel_id=1, source_target_pairs={{0,96},{1,25},{2,98},{3,27},{4,100},{5,29},{6,102},{7,31},{8,104},... | collective-permute-start | bytes 3391496 | tf_op jit(solution)/shard_map/ppermute | solution.py:44
  42.2 27.5 %collective-permute-start.10 = (f32[4,69,8,128]{3,2,1,0:T(8,128)S(1)}, f32[4,69,8,128]{3,2,1,0:T(8,128)S(1)}, u32[]{:S(2)}, u32[]{:S(2)}) collective-permute-start(f32[4,69,8,128]{3,2,1,0:T(8,128)S(1)} %pad_maximum_fusion.refs_0_), channel_id=1, source_target_pairs={{0,1},{1,0},{2,3},{3,2},{4,5},{5,4},{6,7},{7,6},{8,9},{9,8},{10,11... | collective-permute-start | bytes 3391496 | tf_op jit(solution)/shard_map/ppermute | solution.py:31
  53.7 17.6 %collective-permute-start.11 = (f32[4,69,8,128]{3,2,1,0:T(8,128)S(1)}, f32[4,69,8,128]{3,2,1,0:T(8,128)S(1)}, u32[]{:S(2)}, u32[]{:S(2)}) collective-permute-start(f32[4,69,8,128]{3,2,1,0:T(8,128)S(1)} %collective-permute-done.7.refs_1_), channel_id=1, source_target_pairs={{0,1},{1,0},{2,3},{3,2},{4,5},{5,4},{6,7},{7,6},{8,9},{9,8},{10,11... | collective-permute-start | bytes 3391496 | tf_op jit(solution)/shard_map/ppermute | solution.py:31
  56.4 19.0 %copy-start.1 = (f32[1024]{0:T(1024)S(1)}, f32[1024]{0:T(1024)}, u32[]{:S(2)}) copy-start(f32[1024]{0:T(1024)} %param.10) | copy-start | bytes 12292
  66.5 6.1 %collective-permute-start.12 = (f32[4,69,8,128]{3,2,1,0:T(8,128)S(1)}, f32[4,69,8,128]{3,2,1,0:T(8,128)S(1)}, u32[]{:S(2)}, u32[]{:S(2)}) collective-permute-start(f32[4,69,8,128]{3,2,1,0:T(8,128)S(1)} %collective-permute-done.8.refs_2_), channel_id=1, source_target_pairs={{0,1},{1,0},{2,3},{3,2},{4,5},{5,4},{6,7},{7,6},{8,9},{9,8},{10,11... | collective-permute-start | bytes 3391496 | tf_op jit(solution)/shard_map/ppermute | solution.py:31
  69.6 5.7 %collective-permute-start.13 = (f32[4,69,8,128]{3,2,1,0:T(8,128)S(1)}, f32[4,69,8,128]{3,2,1,0:T(8,128)S(1)}, u32[]{:S(2)}, u32[]{:S(2)}) collective-permute-start(f32[4,69,8,128]{3,2,1,0:T(8,128)S(1)} %collective-permute-done.9.refs_3_), channel_id=1, source_target_pairs={{0,1},{1,0},{2,3},{3,2},{4,5},{5,4},{6,7},{7,6},{8,9},{9,8},{10,11... | collective-permute-start | bytes 3391496 | tf_op jit(solution)/shard_map/ppermute | solution.py:31
  69.7 35.6 %collective-permute-start.14 = (f32[4,64,8,128]{3,2,1,0:T(8,128)S(1)}, f32[4,64,8,128]{3,2,1,0:T(8,128)S(1)}, u32[]{:S(2)}, u32[]{:S(2)}) collective-permute-start(f32[4,64,8,128]{3,2,1,0:T(8,128)S(1)} %pad_maximum_fusion.1.refs_0_), channel_id=1, source_target_pairs={{0,32},{1,9},{2,34},{3,11},{4,36},{5,13},{6,38},{7,15},{8,40},{9,1... | collective-permute-start | bytes 3145736 | tf_op jit(solution)/shard_map/ppermute | solution.py:44
  69.8 35.6 %collective-permute-start.15 = (f32[4,64,8,128]{3,2,1,0:T(8,128)S(1)}, f32[4,64,8,128]{3,2,1,0:T(8,128)S(1)}, u32[]{:S(2)}, u32[]{:S(2)}) collective-permute-start(f32[4,64,8,128]{3,2,1,0:T(8,128)S(1)} %pad_maximum_fusion.1.refs_0_), channel_id=1, source_target_pairs={{0,64},{1,17},{2,66},{3,19},{4,68},{5,21},{6,70},{7,23},{8,72},{9,... | collective-permute-start | bytes 3145736 | tf_op jit(solution)/shard_map/ppermute | solution.py:44
  71.3 34.1 %collective-permute-start.16 = (f32[4,64,8,128]{3,2,1,0:T(8,128)S(1)}, f32[4,64,8,128]{3,2,1,0:T(8,128)S(1)}, u32[]{:S(2)}, u32[]{:S(2)}) collective-permute-start(f32[4,64,8,128]{3,2,1,0:T(8,128)S(1)} %pad_maximum_fusion.1.refs_0_), channel_id=1, source_target_pairs={{0,96},{1,25},{2,98},{3,27},{4,100},{5,29},{6,102},{7,31},{8,104},... | collective-permute-start | bytes 3145736 | tf_op jit(solution)/shard_map/ppermute | solution.py:44
  72.5 50.3 %collective-permute-start.17 = (f32[4,64,8,128]{3,2,1,0:T(8,128)S(1)}, f32[4,64,8,128]{3,2,1,0:T(8,128)S(1)}, u32[]{:S(2)}, u32[]{:S(2)}) collective-permute-start(f32[4,64,8,128]{3,2,1,0:T(8,128)S(1)} %pad_maximum_fusion.1.refs_0_), channel_id=1, source_target_pairs={{0,1},{1,0},{2,3},{3,2},{4,5},{5,4},{6,7},{7,6},{8,9},{9,8},{10,11... | collective-permute-start | bytes 3145736 | tf_op jit(solution)/shard_map/ppermute | solution.py:31
  105.4 17.4 %collective-permute-start.18 = (f32[4,64,8,128]{3,2,1,0:T(8,128)S(1)}, f32[4,64,8,128]{3,2,1,0:T(8,128)S(1)}, u32[]{:S(2)}, u32[]{:S(2)}) collective-permute-start(f32[4,64,8,128]{3,2,1,0:T(8,128)S(1)} %collective-permute-done.14.refs_1_), channel_id=1, source_target_pairs={{0,1},{1,0},{2,3},{3,2},{4,5},{5,4},{6,7},{7,6},{8,9},{9,8},{10,11... | collective-permute-start | bytes 3145736 | tf_op jit(solution)/shard_map/ppermute | solution.py:31
  105.5 17.3 %collective-permute-start.19 = (f32[4,64,8,128]{3,2,1,0:T(8,128)S(1)}, f32[4,64,8,128]{3,2,1,0:T(8,128)S(1)}, u32[]{:S(2)}, u32[]{:S(2)}) collective-permute-start(f32[4,64,8,128]{3,2,1,0:T(8,128)S(1)} %collective-permute-done.15.refs_2_), channel_id=1, source_target_pairs={{0,1},{1,0},{2,3},{3,2},{4,5},{5,4},{6,7},{7,6},{8,9},{9,8},{10,11... | collective-permute-start | bytes 3145736 | tf_op jit(solution)/shard_map/ppermute | solution.py:31
  106.0 16.9 %collective-permute-start.20 = (f32[4,64,8,128]{3,2,1,0:T(8,128)S(1)}, f32[4,64,8,128]{3,2,1,0:T(8,128)S(1)}, u32[]{:S(2)}, u32[]{:S(2)}) collective-permute-start(f32[4,64,8,128]{3,2,1,0:T(8,128)S(1)} %collective-permute-done.16.refs_3_), channel_id=1, source_target_pairs={{0,1},{1,0},{2,3},{3,2},{4,5},{5,4},{6,7},{7,6},{8,9},{9,8},{10,11... | collective-permute-start | bytes 3145736 | tf_op jit(solution)/shard_map/ppermute | solution.py:31

commit v2 on v1

--- a/solution.py
+++ b/solution.py
@@ -50,6 +50,10 @@
     return rows.reshape(r // SUB, SUB, n, LANES).transpose(0, 2, 1, 3).reshape(r // SUB * n, SUB, LANES)
 
 
+def wrap(position):
+    return jnp.bitwise_and(position, SIDE - 1)
+
+
 def whereabouts():
     tm = lax.axis_index("tm")
     rows = lax.axis_index("rows")
@@ -60,17 +64,18 @@
     y, x, z, c = place
 
     def move(i, carry):
-        k2 = i // SIDE
-        kz = i % SIDE
-        pz = (z - kz + SIDE) % SIDE
+        k2 = jnp.right_shift(i, SIDE.bit_length() - 1)
+        kz = wrap(i)
+        pz = wrap(z - kz)
         for k3 in range(SIDE):
             for mine in (True, False):
                 q = c if mine else 1 - c
                 dy = jnp.where(q == 0, k3, k2)
                 dx = jnp.where(q == 0, k2, k3)
-                chip = ((y - dy + SIDE) % SIDE * SIDE + (x - dx + SIDE) % SIDE) * SIDE + pz
+                chip = (wrap(y - dy) * SIDE + wrap(x - dx)) * SIDE + pz
                 src = (own if mine else par)[k3]
-                mats[q, pl.ds(chip * blocks, blocks)] = src[k2, pl.ds(kz * blocks, blocks)]
+                there = pl.ds(pl.multiple_of(chip * blocks, blocks), blocks)
+                mats[q, there] = src[k2, pl.ds(pl.multiple_of(kz * blocks, blocks), blocks)]
         return carry
 
     lax.fori_loop(0, SIDE * SIDE, move, 0)
@@ -85,7 +90,7 @@
                 q = c if mine else 1 - c
                 dy = jnp.where(q == 0, k3, k2)
                 dx = jnp.where(q == 0, k2, k3)
-                seg = (y - dy + SIDE) % SIDE * SIDE + (x - dx + SIDE) % SIDE
+                seg = wrap(y - dy) * SIDE + wrap(x - dx)
                 src = (own if mine else par)[k3]
                 inject[pl.ds(seg * 2 * count + q * count, count)] = src[k2, first : first + count]
         return carry
@@ -101,23 +106,22 @@
         for k2 in range(SIDE):
             dy = jnp.where(c == 0, k3, k2)
             dx = jnp.where(c == 0, k2, k3)
-            seg = (y - dy + SIDE) % SIDE * SIDE + (x - dx + SIDE) % SIDE
+            seg = wrap(y - dy) * SIDE + wrap(x - dx)
             flags = jnp.where(lane == sub, own[k3][k2, first], 0.0)
             seen[pl.ds(seg, 1), :] = jnp.sum(flags, 0, keepdims=True)
 
 
 def transpose_matrices(mats, mats_t, groups):
-    def block(i, carry):
-        s = i // (groups * groups)
-        b = i // groups % groups
-        k = i % groups
-        rows = [mats[s, (b * 16 + r) * groups + k] for r in range(16)]
-        flipped = jnp.concatenate(rows, 0).T
-        for r in range(16):
-            mats_t[s, (k * 16 + r) * groups + b] = flipped[r * SUB : (r + 1) * SUB]
+    def block_row(b, carry):
+        for s in range(2):
+            for k in range(groups):
+                rows = [mats[s, (b * 16 + r) * groups + k] for r in range(16)]
+                flipped = jnp.concatenate(rows, 0).T
+                for r in range(16):
+                    mats_t[s, (k * 16 + r) * groups + b] = flipped[r * SUB : (r + 1) * SUB]
         return carry
 
-    lax.fori_loop(0, 2 * groups * groups, block, 0, unroll=16)
+    lax.fori_loop(0, groups, block_row, 0)
 
 
 def run_chain(seen, mats, mats_t, inject, inject_t, start, out, out_t, reverse, begin, count):

time: 166 us -> 164 us (0.988)
  Pallas kernels: 89.6 us -> 87.4 us
where the time goes in v2:
time: 164 us
  Pallas kernels  87.4 us (53%)
  waiting for transfers between devices  38.8 us (24%)
  starting transfers between devices  31 us (19%)
  matrix products  3.43 us (2%)
  other arithmetic  1.67 us (1%)
    pallas_call x1, Pallas kernels, shards(): pl.pallas_call(partial(backward_kernel, groups=groups), out_shape=out_blo...  42 us
    ppermute x9, waiting for transfers between devices, across(): return lax.ppermute(value, ALL, pairs)  33.1 us
    pallas_call x1, Pallas kernels, shards(): pl.pallas_call(partial(first_kernel, groups=groups), out_shape=(shape(fir...  28.7 us
    pallas_call x1, Pallas kernels, shards(): pl.pallas_call(partial(second_kernel, groups=groups), out_shape=(out_bloc...  16.7 us
    ppermute x9, starting transfers between devices, swap_cores(): lax.ppermute(value, ALL, [(device_id(y, x, z, c), device_id(y, x, z, 1 -...  13.8 us
    ppermute x9, starting transfers between devices, across(): return lax.ppermute(value, ALL, pairs)  11.3 us
    ppermute x3, starting transfers between devices, along_z(): lax.ppermute(value, ALL, [(device_id(y, x, z, c), device_id(y, x, z + k,...  5.85 us
    ppermute x3, waiting for transfers between devices, along_z(): lax.ppermute(value, ALL, [(device_id(y, x, z, c), device_id(y, x, z + k,...  5.63 us
  transfers between devices with their start and end apart: 21, of which 6 were waited for; matrix products, arithmetic and copies ran while one was open for 3% of the time, Pallas kernels for 28%

profile of v2, /device:TPU:1, one launch (start us, length us, event | category | flops | bytes accessed | tf_op | source)
XLA Modules:
  0.0 163.7 jit_solution(15756389449248261309)
XLA Ops:
  0.6 0.0 copy-start
  0.7 0.8 fusion.17
  1.5 1.5 collective-permute-start
  2.9 0.7 convert_element_type.3
  3.6 3.4 %fusion.5 = f32[8,512]{1,0:T(8,128)S(1)} fusion(f32[8,1024]{1,0:T(8,128)S(1)} %copy-done, f32[1024,1024]{1,0:T(8,128)} %param.13, s32[]{:T(128)S(6)} %select_n.36, f32[8]{0:T(128)S(1)} %convert_element_type.3), kind=kOutput, calls=%fused_computation.4 | convolution fusion | flops 50335744 | bytes 2146340 | tf_op jit(solution)/shard_map/dot_general | solution.py:283
  7.0 0.0 collective-permute-done
  7.1 1.8 %collective-permute-start.1 = (f32[2,16,8,128]{3,2,1,0:T(8,128)S(1)}, f32[2,16,8,128]{3,2,1,0:T(8,128)S(1)}, u32[]{:S(2)}, u32[]{:S(2)}) collective-permute-start(f32[2,16,8,128]{3,2,1,0:T(8,128)S(1)} %maximum_select_fusion), channel_id=1, source_target_pairs={{0,2},{1,3},{2,4},{3,5},{4,6},{5,7},{6,0},{7,1},{8,10},{9,11},{10,... | collective-permute-start | bytes 393224 | tf_op jit(solution)/shard_map/ppermute | solution.py:35
  8.9 3.3 %collective-permute-start.2 = (f32[2,16,8,128]{3,2,1,0:T(8,128)S(1)}, f32[2,16,8,128]{3,2,1,0:T(8,128)S(1)}, u32[]{:S(2)}, u32[]{:S(2)}) collective-permute-start(f32[2,16,8,128]{3,2,1,0:T(8,128)S(1)} %maximum_select_fusion), channel_id=1, source_target_pairs={{0,4},{1,5},{2,6},{3,7},{4,0},{5,1},{6,2},{7,3},{8,12},{9,13},{10,... | collective-permute-start | bytes 393224 | tf_op jit(solution)/shard_map/ppermute | solution.py:35
  12.2 0.7 collective-permute-start.3
  12.9 1.9 %collective-permute-done.1 = f32[2,16,8,128]{3,2,1,0:T(8,128)S(1)} collective-permute-done((f32[2,16,8,128]{3,2,1,0:T(8,128)S(1)}, f32[2,16,8,128]{3,2,1,0:T(8,128)S(1)}, u32[]{:S(2)}, u32[]{:S(2)}) %collective-permute-start.1) | collective-permute-done | bytes 131104 | tf_op jit(solution)/shard_map/ppermute | solution.py:35
  14.9 3.7 %collective-permute-done.2 = f32[2,16,8,128]{3,2,1,0:T(8,128)S(1)} collective-permute-done((f32[2,16,8,128]{3,2,1,0:T(8,128)S(1)}, f32[2,16,8,128]{3,2,1,0:T(8,128)S(1)}, u32[]{:S(2)}, u32[]{:S(2)}) %collective-permute-start.2) | collective-permute-done | bytes 131104 | tf_op jit(solution)/shard_map/ppermute | solution.py:35
  18.6 0.0 collective-permute-done.3
  18.6 0.1 constant_dynamic-update-slice_fusion.6
  18.8 2.8 %collective-permute-start.6 = (f32[133,8,128]{2,1,0:T(8,128)S(1)}, f32[133,8,128]{2,1,0:T(8,128)S(1)}, u32[]{:S(2)}, u32[]{:S(2)}) collective-permute-start(f32[133,8,128]{2,1,0:T(8,128)S(1)} %get-tuple-element.29), channel_id=1, source_target_pairs={{0,24},{1,97},{2,26},{3,99},{4,28},{5,101},{6,30},{7,103},{8,0},{9... | collective-permute-start | bytes 1634312 | tf_op jit(solution)/shard_map/ppermute | solution.py:44
  21.6 0.3 collective-permute-start.5
  21.9 0.7 collective-permute-start.4
  22.6 0.1 constant_dynamic-update-slice_fusion
  22.7 11.1 %collective-permute-done.6 = f32[133,8,128]{2,1,0:T(8,128)S(1)} collective-permute-done((f32[133,8,128]{2,1,0:T(8,128)S(1)}, f32[133,8,128]{2,1,0:T(8,128)S(1)}, u32[]{:S(2)}, u32[]{:S(2)}) %collective-permute-start.6) | collective-permute-done | bytes 544800 | tf_op jit(solution)/shard_map/ppermute | solution.py:44
  33.8 0.0 collective-permute-done.5
  33.8 3.6 %collective-permute-done.4 = f32[133,8,128]{2,1,0:T(8,128)S(1)} collective-permute-done((f32[133,8,128]{2,1,0:T(8,128)S(1)}, f32[133,8,128]{2,1,0:T(8,128)S(1)}, u32[]{:S(2)}, u32[]{:S(2)}) %collective-permute-start.4) | collective-permute-done | bytes 544800 | tf_op jit(solution)/shard_map/ppermute | solution.py:44
  37.5 0.1 pad_maximum_fusion.refs_0_
  37.5 1.0 collective-permute-start.7
  38.5 2.5 %collective-permute-start.8 = (f32[4,69,8,128]{3,2,1,0:T(8,128)S(1)}, f32[4,69,8,128]{3,2,1,0:T(8,128)S(1)}, u32[]{:S(2)}, u32[]{:S(2)}) collective-permute-start(f32[4,69,8,128]{3,2,1,0:T(8,128)S(1)} %pad_maximum_fusion.refs_0_), channel_id=1, source_target_pairs={{0,64},{1,17},{2,66},{3,19},{4,68},{5,21},{6,70},{7,23},{8,72},{9,... | collective-permute-start | bytes 3391496 | tf_op jit(solution)/shard_map/ppermute | solution.py:44
  41.1 1.2 collective-permute-start.9
  42.2 3.1 %collective-permute-start.10 = (f32[4,69,8,128]{3,2,1,0:T(8,128)S(1)}, f32[4,69,8,128]{3,2,1,0:T(8,128)S(1)}, u32[]{:S(2)}, u32[]{:S(2)}) collective-permute-start(f32[4,69,8,128]{3,2,1,0:T(8,128)S(1)} %pad_maximum_fusion.refs_0_), channel_id=1, source_target_pairs={{0,1},{1,0},{2,3},{3,2},{4,5},{5,4},{6,7},{7,6},{8,9},{9,8},{10,11... | collective-permute-start | bytes 3391496 | tf_op jit(solution)/shard_map/ppermute | solution.py:31
  45.3 8.3 %collective-permute-done.7.refs_1_ = f32[4,69,8,128]{3,2,1,0:T(8,128)S(1)} collective-permute-done((f32[4,69,8,128]{3,2,1,0:T(8,128)S(1)}, f32[4,69,8,128]{3,2,1,0:T(8,128)S(1)}, u32[]{:S(2)}, u32[]{:S(2)}) %collective-permute-start.7) | collective-permute-done | bytes 1130528 | tf_op jit(solution)/shard_map/ppermute | solution.py:44
  53.7 2.6 %collective-permute-start.11 = (f32[4,69,8,128]{3,2,1,0:T(8,128)S(1)}, f32[4,69,8,128]{3,2,1,0:T(8,128)S(1)}, u32[]{:S(2)}, u32[]{:S(2)}) collective-permute-start(f32[4,69,8,128]{3,2,1,0:T(8,128)S(1)} %collective-permute-done.7.refs_1_), channel_id=1, source_target_pairs={{0,1},{1,0},{2,3},{3,2},{4,5},{5,4},{6,7},{7,6},{8,9},{9,8},{10,11... | collective-permute-start | bytes 3391496 | tf_op jit(solution)/shard_map/ppermute | solution.py:31
  56.4 0.0 copy-start.1
  56.4 10.1 %collective-permute-done.8.refs_2_ = f32[4,69,8,128]{3,2,1,0:T(8,128)S(1)} collective-permute-done((f32[4,69,8,128]{3,2,1,0:T(8,128)S(1)}, f32[4,69,8,128]{3,2,1,0:T(8,128)S(1)}, u32[]{:S(2)}, u32[]{:S(2)}) %collective-permute-start.8) | collective-permute-done | bytes 1130528 | tf_op jit(solution)/shard_map/ppermute | solution.py:44
  66.5 3.2 %collective-permute-start.12 = (f32[4,69,8,128]{3,2,1,0:T(8,128)S(1)}, f32[4,69,8,128]{3,2,1,0:T(8,128)S(1)}, u32[]{:S(2)}, u32[]{:S(2)}) collective-permute-start(f32[4,69,8,128]{3,2,1,0:T(8,128)S(1)} %collective-permute-done.8.refs_2_), channel_id=1, source_target_pairs={{0,1},{1,0},{2,3},{3,2},{4,5},{5,4},{6,7},{7,6},{8,9},{9,8},{10,11... | collective-permute-start | bytes 3391496 | tf_op jit(solution)/shard_map/ppermute | solution.py:31
  69.6 0.0 collective-permute-done.9.refs_3_
  69.6 0.0 collective-permute-start.13
  69.6 0.1 pad_maximum_fusion.1.refs_0_
  69.7 0.1 collective-permute-start.14
  69.8 1.5 collective-permute-start.15
  71.3 1.2 collective-permute-start.16
  72.5 2.8 %collective-permute-start.17 = (f32[4,64,8,128]{3,2,1,0:T(8,128)S(1)}, f32[4,64,8,128]{3,2,1,0:T(8,128)S(1)}, u32[]{:S(2)}, u32[]{:S(2)}) collective-permute-start(f32[4,64,8,128]{3,2,1,0:T(8,128)S(1)} %pad_maximum_fusion.1.refs_0_), channel_id=1, source_target_pairs={{0,1},{1,0},{2,3},{3,2},{4,5},{5,4},{6,7},{7,6},{8,9},{9,8},{10,11... | collective-permute-start | bytes 3145736 | tf_op jit(solution)/shard_map/ppermute | solution.py:31
  75.4 0.0 collective-permute-done.13.refs_7_
  75.4 28.7 %forward_first.1 = (f32[80,1024]{1,0:T(8,128)S(1)}, f32[2,1024,8,128]{3,2,1,0:T(8,128)S(1)}, f32[2,1024,8,128]{3,2,1,0:T(8,128)S(1)}, f32[128,1024]{1,0:T(8,128)...) custom-call(f32[1,1024]{1,0:T(1,128)S(1)} %bitcast.78, f32[4,69,8,128]{3,2,1,0:T(8,128)S(1)} %pad_maximum_fusion.refs_0_, ...), custom_call_target="tpu_custom_call" | custom-call | tf_op jit(solution)/shard_map/forward_first/pallas_call | solution.py:314
  104.1 0.0 collective-permute-done.15.refs_2_
  104.1 0.0 collective-permute-done.16.refs_3_
  104.1 0.1 collective-permute-start.18
  104.2 0.5 collective-permute-start.19
  104.7 0.1 collective-permute-start.20
  104.8 16.7 %forward_second.1 = (f32[8,128]{1,0:T(8,128)}, f32[128,1024]{1,0:T(8,128)S(1)}, f32[128,1024]{1,0:T(8,128)S(1)}) custom-call(f32[16,128]{1,0:T(8,128)S(1)} %get-tuple-element.15.seen, f32[80,1024]{1,0:T(8,128)S(1)} %get-tuple-element.17.earlier, f32[2,1024,8,128]{3,2,1,0:T(8,128)S(1)} %get-tuple-element.18.mats, ...), custom_call_target="tpu_custom_call" | custom-call | tf_op jit(solution)/shard_map/forward_second/pallas_call | solution.py:334
  121.5 0.0 collective-permute-done.18.refs_5_
  121.5 0.0 collective-permute-done.19.refs_6_
  121.6 42.0 %backward_chain.1 = f32[8,128]{1,0:T(8,128)} custom-call(f32[16,128]{1,0:T(8,128)S(1)} %get-tuple-element.15.seen, f32[128,1024]{1,0:T(8,128)S(1)} %get-tuple-element.23.error, f32[128,1024]{1,0:T(8,128)S(1)} %get-tuple-element.24.prior, f32[4,64,8,128]{3,2,1,0:T(8,128)S(1)} %pad_maximum_fusion.1.refs_0_, ...), custom_call_target="tpu_custom_call" | custom-call | tf_op jit(solution)/shard_map/backward_chain/pallas_call | solution.py:344
  (30 shorter events, 0.3 us)
Async XLA Ops:
  0.6 3.0 %copy-start = (f32[8,1024]{1,0:T(8,128)S(1)}, f32[8,1024]{1,0:T(8,128)}, u32[]{:S(2)}) copy-start(f32[8,1024]{1,0:T(8,128)} %param.8) | copy-start | bytes 98308
  1.5 5.6 %collective-permute-start = (f32[2,8,8,128]{3,2,1,0:T(8,128)S(1)}, f32[2,8,8,128]{3,2,1,0:T(8,128)S(1)}, u32[]{:S(2)}, u32[]{:S(2)}) collective-permute-start(f32[2,8,8,128]{3,2,1,0:T(8,128)S(1)} %get-tuple-element.37), channel_id=1, source_target_pairs={{0,1},{1,0},{2,3},{3,2},{4,5},{5,4},{6,7},{7,6},{8,9},{9,8},{10,11... | collective-permute-start | bytes 196616 | tf_op jit(solution)/shard_map/ppermute | solution.py:31
  7.1 7.8 %collective-permute-start.1 = (f32[2,16,8,128]{3,2,1,0:T(8,128)S(1)}, f32[2,16,8,128]{3,2,1,0:T(8,128)S(1)}, u32[]{:S(2)}, u32[]{:S(2)}) collective-permute-start(f32[2,16,8,128]{3,2,1,0:T(8,128)S(1)} %maximum_select_fusion), channel_id=1, source_target_pairs={{0,2},{1,3},{2,4},{3,5},{4,6},{5,7},{6,0},{7,1},{8,10},{9,11},{10,... | collective-permute-start | bytes 393224 | tf_op jit(solution)/shard_map/ppermute | solution.py:35
  8.9 9.7 %collective-permute-start.2 = (f32[2,16,8,128]{3,2,1,0:T(8,128)S(1)}, f32[2,16,8,128]{3,2,1,0:T(8,128)S(1)}, u32[]{:S(2)}, u32[]{:S(2)}) collective-permute-start(f32[2,16,8,128]{3,2,1,0:T(8,128)S(1)} %maximum_select_fusion), channel_id=1, source_target_pairs={{0,4},{1,5},{2,6},{3,7},{4,0},{5,1},{6,2},{7,3},{8,12},{9,13},{10,... | collective-permute-start | bytes 393224 | tf_op jit(solution)/shard_map/ppermute | solution.py:35
  12.2 6.4 %collective-permute-start.3 = (f32[2,16,8,128]{3,2,1,0:T(8,128)S(1)}, f32[2,16,8,128]{3,2,1,0:T(8,128)S(1)}, u32[]{:S(2)}, u32[]{:S(2)}) collective-permute-start(f32[2,16,8,128]{3,2,1,0:T(8,128)S(1)} %maximum_select_fusion), channel_id=1, source_target_pairs={{0,6},{1,7},{2,0},{3,1},{4,2},{5,3},{6,4},{7,5},{8,14},{9,15},{10,... | collective-permute-start | bytes 393224 | tf_op jit(solution)/shard_map/ppermute | solution.py:35
  18.8 15.0 %collective-permute-start.6 = (f32[133,8,128]{2,1,0:T(8,128)S(1)}, f32[133,8,128]{2,1,0:T(8,128)S(1)}, u32[]{:S(2)}, u32[]{:S(2)}) collective-permute-start(f32[133,8,128]{2,1,0:T(8,128)S(1)} %get-tuple-element.29), channel_id=1, source_target_pairs={{0,24},{1,97},{2,26},{3,99},{4,28},{5,101},{6,30},{7,103},{8,0},{9... | collective-permute-start | bytes 1634312 | tf_op jit(solution)/shard_map/ppermute | solution.py:44
  21.6 12.2 %collective-permute-start.5 = (f32[133,8,128]{2,1,0:T(8,128)S(1)}, f32[133,8,128]{2,1,0:T(8,128)S(1)}, u32[]{:S(2)}, u32[]{:S(2)}) collective-permute-start(f32[133,8,128]{2,1,0:T(8,128)S(1)} %get-tuple-element.29), channel_id=1, source_target_pairs={{0,16},{1,65},{2,18},{3,67},{4,20},{5,69},{6,22},{7,71},{8,24},{9,... | collective-permute-start | bytes 1634312 | tf_op jit(solution)/shard_map/ppermute | solution.py:44
  21.9 15.5 %collective-permute-start.4 = (f32[133,8,128]{2,1,0:T(8,128)S(1)}, f32[133,8,128]{2,1,0:T(8,128)S(1)}, u32[]{:S(2)}, u32[]{:S(2)}) collective-permute-start(f32[133,8,128]{2,1,0:T(8,128)S(1)} %get-tuple-element.29), channel_id=1, source_target_pairs={{0,8},{1,33},{2,10},{3,35},{4,12},{5,37},{6,14},{7,39},{8,16},{9,4... | collective-permute-start | bytes 1634312 | tf_op jit(solution)/shard_map/ppermute | solution.py:44
  37.5 16.1 %collective-permute-start.7 = (f32[4,69,8,128]{3,2,1,0:T(8,128)S(1)}, f32[4,69,8,128]{3,2,1,0:T(8,128)S(1)}, u32[]{:S(2)}, u32[]{:S(2)}) collective-permute-start(f32[4,69,8,128]{3,2,1,0:T(8,128)S(1)} %pad_maximum_fusion.refs_0_), channel_id=1, source_target_pairs={{0,32},{1,9},{2,34},{3,11},{4,36},{5,13},{6,38},{7,15},{8,40},{9,1... | collective-permute-start | bytes 3391496 | tf_op jit(solution)/shard_map/ppermute | solution.py:44
  38.5 27.9 %collective-permute-start.8 = (f32[4,69,8,128]{3,2,1,0:T(8,128)S(1)}, f32[4,69,8,128]{3,2,1,0:T(8,128)S(1)}, u32[]{:S(2)}, u32[]{:S(2)}) collective-permute-start(f32[4,69,8,128]{3,2,1,0:T(8,128)S(1)} %pad_maximum_fusion.refs_0_), channel_id=1, source_target_pairs={{0,64},{1,17},{2,66},{3,19},{4,68},{5,21},{6,70},{7,23},{8,72},{9,... | collective-permute-start | bytes 3391496 | tf_op jit(solution)/shard_map/ppermute | solution.py:44
  41.1 28.5 %collective-permute-start.9 = (f32[4,69,8,128]{3,2,1,0:T(8,128)S(1)}, f32[4,69,8,128]{3,2,1,0:T(8,128)S(1)}, u32[]{:S(2)}, u32[]{:S(2)}) collective-permute-start(f32[4,69,8,128]{3,2,1,0:T(8,128)S(1)} %pad_maximum_fusion.refs_0_), channel_id=1, source_target_pairs={{0,96},{1,25},{2,98},{3,27},{4,100},{5,29},{6,102},{7,31},{8,104},... | collective-permute-start | bytes 3391496 | tf_op jit(solution)/shard_map/ppermute | solution.py:44
  42.2 27.5 %collective-permute-start.10 = (f32[4,69,8,128]{3,2,1,0:T(8,128)S(1)}, f32[4,69,8,128]{3,2,1,0:T(8,128)S(1)}, u32[]{:S(2)}, u32[]{:S(2)}) collective-permute-start(f32[4,69,8,128]{3,2,1,0:T(8,128)S(1)} %pad_maximum_fusion.refs_0_), channel_id=1, source_target_pairs={{0,1},{1,0},{2,3},{3,2},{4,5},{5,4},{6,7},{7,6},{8,9},{9,8},{10,11... | collective-permute-start | bytes 3391496 | tf_op jit(solution)/shard_map/ppermute | solution.py:31
  53.7 17.6 %collective-permute-start.11 = (f32[4,69,8,128]{3,2,1,0:T(8,128)S(1)}, f32[4,69,8,128]{3,2,1,0:T(8,128)S(1)}, u32[]{:S(2)}, u32[]{:S(2)}) collective-permute-start(f32[4,69,8,128]{3,2,1,0:T(8,128)S(1)} %collective-permute-done.7.refs_1_), channel_id=1, source_target_pairs={{0,1},{1,0},{2,3},{3,2},{4,5},{5,4},{6,7},{7,6},{8,9},{9,8},{10,11... | collective-permute-start | bytes 3391496 | tf_op jit(solution)/shard_map/ppermute | solution.py:31
  56.4 19.0 %copy-start.1 = (f32[1024]{0:T(1024)S(1)}, f32[1024]{0:T(1024)}, u32[]{:S(2)}) copy-start(f32[1024]{0:T(1024)} %param.10) | copy-start | bytes 12292
  66.5 6.1 %collective-permute-start.12 = (f32[4,69,8,128]{3,2,1,0:T(8,128)S(1)}, f32[4,69,8,128]{3,2,1,0:T(8,128)S(1)}, u32[]{:S(2)}, u32[]{:S(2)}) collective-permute-start(f32[4,69,8,128]{3,2,1,0:T(8,128)S(1)} %collective-permute-done.8.refs_2_), channel_id=1, source_target_pairs={{0,1},{1,0},{2,3},{3,2},{4,5},{5,4},{6,7},{7,6},{8,9},{9,8},{10,11... | collective-permute-start | bytes 3391496 | tf_op jit(solution)/shard_map/ppermute | solution.py:31
  69.6 5.7 %collective-permute-start.13 = (f32[4,69,8,128]{3,2,1,0:T(8,128)S(1)}, f32[4,69,8,128]{3,2,1,0:T(8,128)S(1)}, u32[]{:S(2)}, u32[]{:S(2)}) collective-permute-start(f32[4,69,8,128]{3,2,1,0:T(8,128)S(1)} %collective-permute-done.9.refs_3_), channel_id=1, source_target_pairs={{0,1},{1,0},{2,3},{3,2},{4,5},{5,4},{6,7},{7,6},{8,9},{9,8},{10,11... | collective-permute-start | bytes 3391496 | tf_op jit(solution)/shard_map/ppermute | solution.py:31
  69.7 34.4 %collective-permute-start.14 = (f32[4,64,8,128]{3,2,1,0:T(8,128)S(1)}, f32[4,64,8,128]{3,2,1,0:T(8,128)S(1)}, u32[]{:S(2)}, u32[]{:S(2)}) collective-permute-start(f32[4,64,8,128]{3,2,1,0:T(8,128)S(1)} %pad_maximum_fusion.1.refs_0_), channel_id=1, source_target_pairs={{0,32},{1,9},{2,34},{3,11},{4,36},{5,13},{6,38},{7,15},{8,40},{9,1... | collective-permute-start | bytes 3145736 | tf_op jit(solution)/shard_map/ppermute | solution.py:44
  69.8 34.3 %collective-permute-start.15 = (f32[4,64,8,128]{3,2,1,0:T(8,128)S(1)}, f32[4,64,8,128]{3,2,1,0:T(8,128)S(1)}, u32[]{:S(2)}, u32[]{:S(2)}) collective-permute-start(f32[4,64,8,128]{3,2,1,0:T(8,128)S(1)} %pad_maximum_fusion.1.refs_0_), channel_id=1, source_target_pairs={{0,64},{1,17},{2,66},{3,19},{4,68},{5,21},{6,70},{7,23},{8,72},{9,... | collective-permute-start | bytes 3145736 | tf_op jit(solution)/shard_map/ppermute | solution.py:44
  71.3 32.8 %collective-permute-start.16 = (f32[4,64,8,128]{3,2,1,0:T(8,128)S(1)}, f32[4,64,8,128]{3,2,1,0:T(8,128)S(1)}, u32[]{:S(2)}, u32[]{:S(2)}) collective-permute-start(f32[4,64,8,128]{3,2,1,0:T(8,128)S(1)} %pad_maximum_fusion.1.refs_0_), channel_id=1, source_target_pairs={{0,96},{1,25},{2,98},{3,27},{4,100},{5,29},{6,102},{7,31},{8,104},... | collective-permute-start | bytes 3145736 | tf_op jit(solution)/shard_map/ppermute | solution.py:44
  72.5 49.0 %collective-permute-start.17 = (f32[4,64,8,128]{3,2,1,0:T(8,128)S(1)}, f32[4,64,8,128]{3,2,1,0:T(8,128)S(1)}, u32[]{:S(2)}, u32[]{:S(2)}) collective-permute-start(f32[4,64,8,128]{3,2,1,0:T(8,128)S(1)} %pad_maximum_fusion.1.refs_0_), channel_id=1, source_target_pairs={{0,1},{1,0},{2,3},{3,2},{4,5},{5,4},{6,7},{7,6},{8,9},{9,8},{10,11... | collective-permute-start | bytes 3145736 | tf_op jit(solution)/shard_map/ppermute | solution.py:31
  104.1 17.4 %collective-permute-start.18 = (f32[4,64,8,128]{3,2,1,0:T(8,128)S(1)}, f32[4,64,8,128]{3,2,1,0:T(8,128)S(1)}, u32[]{:S(2)}, u32[]{:S(2)}) collective-permute-start(f32[4,64,8,128]{3,2,1,0:T(8,128)S(1)} %collective-permute-done.14.refs_1_), channel_id=1, source_target_pairs={{0,1},{1,0},{2,3},{3,2},{4,5},{5,4},{6,7},{7,6},{8,9},{9,8},{10,11... | collective-permute-start | bytes 3145736 | tf_op jit(solution)/shard_map/ppermute | solution.py:31
  104.2 17.3 %collective-permute-start.19 = (f32[4,64,8,128]{3,2,1,0:T(8,128)S(1)}, f32[4,64,8,128]{3,2,1,0:T(8,128)S(1)}, u32[]{:S(2)}, u32[]{:S(2)}) collective-permute-start(f32[4,64,8,128]{3,2,1,0:T(8,128)S(1)} %collective-permute-done.15.refs_2_), channel_id=1, source_target_pairs={{0,1},{1,0},{2,3},{3,2},{4,5},{5,4},{6,7},{7,6},{8,9},{9,8},{10,11... | collective-permute-start | bytes 3145736 | tf_op jit(solution)/shard_map/ppermute | solution.py:31
  104.7 16.9 %collective-permute-start.20 = (f32[4,64,8,128]{3,2,1,0:T(8,128)S(1)}, f32[4,64,8,128]{3,2,1,0:T(8,128)S(1)}, u32[]{:S(2)}, u32[]{:S(2)}) collective-permute-start(f32[4,64,8,128]{3,2,1,0:T(8,128)S(1)} %collective-permute-done.16.refs_3_), channel_id=1, source_target_pairs={{0,1},{1,0},{2,3},{3,2},{4,5},{5,4},{6,7},{7,6},{8,9},{9,8},{10,11... | collective-permute-start | bytes 3145736 | tf_op jit(solution)/shard_map/ppermute | solution.py:31

commit v3 on v2

--- a/solution.py
+++ b/solution.py
@@ -131,12 +131,20 @@
     lane = lax.broadcasted_iota(jnp.int32, (SUB, LANES), 1)
 
     def pick(t):
-        return (seen[t // SUB, t % SUB] > 0.5).astype(jnp.int32)
-
-    def pair(p, row):
+        return (seen[jnp.right_shift(t, SUB.bit_length() - 1), jnp.bitwise_and(t, SUB - 1)] > 0.5).astype(jnp.int32)
+
+    def times_of(p):
         first = steps - 1 - begin - 2 * p if reverse else begin + 2 * p
-        second = first - 1 if reverse else first + 1
-        s0, s1 = pick(first), pick(second)
+        return first, first - 1 if reverse else first + 1
+
+    def picks(p):
+        first, second = times_of(p)
+        return pick(first), pick(second)
+
+    def pair(p, carry):
+        row, s0, s1 = carry
+        first, second = times_of(p)
+        upcoming = picks(jnp.minimum(p + 1, count // 2 - 1))
         here = lane == first
         state = [jnp.broadcast_to(row[:, k * LANES : (k + 1) * LANES], (SUB, LANES)) for k in range(groups)]
 
@@ -156,9 +164,9 @@
         sums = lax.fori_loop(0, row_blocks, rows, zero, unroll=UNROLL)
         row = jnp.concatenate([jnp.sum(v, 0, keepdims=True) for v in sums], 1) + inject[pl.ds(second, 1), :]
         out[pl.ds(second, 1), :] = row
-        return row
-
-    lax.fori_loop(0, count // 2, pair, start)
+        return row, *upcoming
+
+    lax.fori_loop(0, count // 2, pair, (start, *picks(0)))
     low = steps - begin - count if reverse else begin
     odd = lax.broadcasted_iota(jnp.int32, (count, LANES), 0) % 2
     from_t = odd == (1 if reverse else 0)

time: 164 us -> 163 us (level)
  no operation moved by 1% of the time
where the time goes in v3:
time: 163 us
  Pallas kernels  86.7 us (53%)
  waiting for transfers between devices  38.8 us (24%)
  starting transfers between devices  31 us (19%)
  matrix products  3.43 us (2%)
  other arithmetic  1.67 us (1%)
    pallas_call x1, Pallas kernels, shards(): pl.pallas_call(partial(backward_kernel, groups=groups), out_shape=out_blo...  41.5 us
    ppermute x9, waiting for transfers between devices, across(): return lax.ppermute(value, ALL, pairs)  33.1 us
    pallas_call x1, Pallas kernels, shards(): pl.pallas_call(partial(first_kernel, groups=groups), out_shape=(shape(fir...  28.6 us
    pallas_call x1, Pallas kernels, shards(): pl.pallas_call(partial(second_kernel, groups=groups), out_shape=(out_bloc...  16.6 us
    ppermute x9, starting transfers between devices, swap_cores(): lax.ppermute(value, ALL, [(device_id(y, x, z, c), device_id(y, x, z, 1 -...  13.8 us
    ppermute x9, starting transfers between devices, across(): return lax.ppermute(value, ALL, pairs)  11.3 us
    ppermute x3, starting transfers between devices, along_z(): lax.ppermute(value, ALL, [(device_id(y, x, z, c), device_id(y, x, z + k,...  5.85 us
    ppermute x3, waiting for transfers between devices, along_z(): lax.ppermute(value, ALL, [(device_id(y, x, z, c), device_id(y, x, z + k,...  5.63 us
  transfers between devices with their start and end apart: 21, of which 6 were waited for; matrix products, arithmetic and copies ran while one was open for 3% of the time, Pallas kernels for 28%

profile of v3, /device:TPU:1, one launch (start us, length us, event | category | flops | bytes accessed | tf_op | source)
XLA Modules:
  0.0 163.0 jit_solution(8110604275578316795)
XLA Ops:
  0.6 0.0 copy-start
  0.7 0.8 fusion.17
  1.5 1.5 collective-permute-start
  2.9 0.7 convert_element_type.3
  3.6 3.4 %fusion.5 = f32[8,512]{1,0:T(8,128)S(1)} fusion(f32[8,1024]{1,0:T(8,128)S(1)} %copy-done, f32[1024,1024]{1,0:T(8,128)} %param.13, s32[]{:T(128)S(6)} %select_n.36, f32[8]{0:T(128)S(1)} %convert_element_type.3), kind=kOutput, calls=%fused_computation.4 | convolution fusion | flops 50335744 | bytes 2146340 | tf_op jit(solution)/shard_map/dot_general | solution.py:291
  7.0 0.0 collective-permute-done
  7.1 1.8 %collective-permute-start.1 = (f32[2,16,8,128]{3,2,1,0:T(8,128)S(1)}, f32[2,16,8,128]{3,2,1,0:T(8,128)S(1)}, u32[]{:S(2)}, u32[]{:S(2)}) collective-permute-start(f32[2,16,8,128]{3,2,1,0:T(8,128)S(1)} %maximum_select_fusion), channel_id=1, source_target_pairs={{0,2},{1,3},{2,4},{3,5},{4,6},{5,7},{6,0},{7,1},{8,10},{9,11},{10,... | collective-permute-start | bytes 393224 | tf_op jit(solution)/shard_map/ppermute | solution.py:35
  8.9 3.3 %collective-permute-start.2 = (f32[2,16,8,128]{3,2,1,0:T(8,128)S(1)}, f32[2,16,8,128]{3,2,1,0:T(8,128)S(1)}, u32[]{:S(2)}, u32[]{:S(2)}) collective-permute-start(f32[2,16,8,128]{3,2,1,0:T(8,128)S(1)} %maximum_select_fusion), channel_id=1, source_target_pairs={{0,4},{1,5},{2,6},{3,7},{4,0},{5,1},{6,2},{7,3},{8,12},{9,13},{10,... | collective-permute-start | bytes 393224 | tf_op jit(solution)/shard_map/ppermute | solution.py:35
  12.2 0.7 collective-permute-start.3
  12.9 1.9 %collective-permute-done.1 = f32[2,16,8,128]{3,2,1,0:T(8,128)S(1)} collective-permute-done((f32[2,16,8,128]{3,2,1,0:T(8,128)S(1)}, f32[2,16,8,128]{3,2,1,0:T(8,128)S(1)}, u32[]{:S(2)}, u32[]{:S(2)}) %collective-permute-start.1) | collective-permute-done | bytes 131104 | tf_op jit(solution)/shard_map/ppermute | solution.py:35
  14.9 3.7 %collective-permute-done.2 = f32[2,16,8,128]{3,2,1,0:T(8,128)S(1)} collective-permute-done((f32[2,16,8,128]{3,2,1,0:T(8,128)S(1)}, f32[2,16,8,128]{3,2,1,0:T(8,128)S(1)}, u32[]{:S(2)}, u32[]{:S(2)}) %collective-permute-start.2) | collective-permute-done | bytes 131104 | tf_op jit(solution)/shard_map/ppermute | solution.py:35
  18.6 0.0 collective-permute-done.3
  18.6 0.1 constant_dynamic-update-slice_fusion.6
  18.8 2.8 %collective-permute-start.6 = (f32[133,8,128]{2,1,0:T(8,128)S(1)}, f32[133,8,128]{2,1,0:T(8,128)S(1)}, u32[]{:S(2)}, u32[]{:S(2)}) collective-permute-start(f32[133,8,128]{2,1,0:T(8,128)S(1)} %get-tuple-element.29), channel_id=1, source_target_pairs={{0,24},{1,97},{2,26},{3,99},{4,28},{5,101},{6,30},{7,103},{8,0},{9... | collective-permute-start | bytes 1634312 | tf_op jit(solution)/shard_map/ppermute | solution.py:44
  21.6 0.3 collective-permute-start.5
  21.9 0.7 collective-permute-start.4
  22.6 0.1 constant_dynamic-update-slice_fusion
  22.7 11.1 %collective-permute-done.6 = f32[133,8,128]{2,1,0:T(8,128)S(1)} collective-permute-done((f32[133,8,128]{2,1,0:T(8,128)S(1)}, f32[133,8,128]{2,1,0:T(8,128)S(1)}, u32[]{:S(2)}, u32[]{:S(2)}) %collective-permute-start.6) | collective-permute-done | bytes 544800 | tf_op jit(solution)/shard_map/ppermute | solution.py:44
  33.8 0.0 collective-permute-done.5
  33.8 3.6 %collective-permute-done.4 = f32[133,8,128]{2,1,0:T(8,128)S(1)} collective-permute-done((f32[133,8,128]{2,1,0:T(8,128)S(1)}, f32[133,8,128]{2,1,0:T(8,128)S(1)}, u32[]{:S(2)}, u32[]{:S(2)}) %collective-permute-start.4) | collective-permute-done | bytes 544800 | tf_op jit(solution)/shard_map/ppermute | solution.py:44
  37.5 0.1 pad_maximum_fusion.refs_0_
  37.5 1.0 collective-permute-start.7
  38.5 2.5 %collective-permute-start.8 = (f32[4,69,8,128]{3,2,1,0:T(8,128)S(1)}, f32[4,69,8,128]{3,2,1,0:T(8,128)S(1)}, u32[]{:S(2)}, u32[]{:S(2)}) collective-permute-start(f32[4,69,8,128]{3,2,1,0:T(8,128)S(1)} %pad_maximum_fusion.refs_0_), channel_id=1, source_target_pairs={{0,64},{1,17},{2,66},{3,19},{4,68},{5,21},{6,70},{7,23},{8,72},{9,... | collective-permute-start | bytes 3391496 | tf_op jit(solution)/shard_map/ppermute | solution.py:44
  41.1 1.2 collective-permute-start.9
  42.2 3.1 %collective-permute-start.10 = (f32[4,69,8,128]{3,2,1,0:T(8,128)S(1)}, f32[4,69,8,128]{3,2,1,0:T(8,128)S(1)}, u32[]{:S(2)}, u32[]{:S(2)}) collective-permute-start(f32[4,69,8,128]{3,2,1,0:T(8,128)S(1)} %pad_maximum_fusion.refs_0_), channel_id=1, source_target_pairs={{0,1},{1,0},{2,3},{3,2},{4,5},{5,4},{6,7},{7,6},{8,9},{9,8},{10,11... | collective-permute-start | bytes 3391496 | tf_op jit(solution)/shard_map/ppermute | solution.py:31
  45.3 8.3 %collective-permute-done.7.refs_1_ = f32[4,69,8,128]{3,2,1,0:T(8,128)S(1)} collective-permute-done((f32[4,69,8,128]{3,2,1,0:T(8,128)S(1)}, f32[4,69,8,128]{3,2,1,0:T(8,128)S(1)}, u32[]{:S(2)}, u32[]{:S(2)}) %collective-permute-start.7) | collective-permute-done | bytes 1130528 | tf_op jit(solution)/shard_map/ppermute | solution.py:44
  53.7 2.6 %collective-permute-start.11 = (f32[4,69,8,128]{3,2,1,0:T(8,128)S(1)}, f32[4,69,8,128]{3,2,1,0:T(8,128)S(1)}, u32[]{:S(2)}, u32[]{:S(2)}) collective-permute-start(f32[4,69,8,128]{3,2,1,0:T(8,128)S(1)} %collective-permute-done.7.refs_1_), channel_id=1, source_target_pairs={{0,1},{1,0},{2,3},{3,2},{4,5},{5,4},{6,7},{7,6},{8,9},{9,8},{10,11... | collective-permute-start | bytes 3391496 | tf_op jit(solution)/shard_map/ppermute | solution.py:31
  56.4 0.0 copy-start.1
  56.4 10.1 %collective-permute-done.8.refs_2_ = f32[4,69,8,128]{3,2,1,0:T(8,128)S(1)} collective-permute-done((f32[4,69,8,128]{3,2,1,0:T(8,128)S(1)}, f32[4,69,8,128]{3,2,1,0:T(8,128)S(1)}, u32[]{:S(2)}, u32[]{:S(2)}) %collective-permute-start.8) | collective-permute-done | bytes 1130528 | tf_op jit(solution)/shard_map/ppermute | solution.py:44
  66.5 3.2 %collective-permute-start.12 = (f32[4,69,8,128]{3,2,1,0:T(8,128)S(1)}, f32[4,69,8,128]{3,2,1,0:T(8,128)S(1)}, u32[]{:S(2)}, u32[]{:S(2)}) collective-permute-start(f32[4,69,8,128]{3,2,1,0:T(8,128)S(1)} %collective-permute-done.8.refs_2_), channel_id=1, source_target_pairs={{0,1},{1,0},{2,3},{3,2},{4,5},{5,4},{6,7},{7,6},{8,9},{9,8},{10,11... | collective-permute-start | bytes 3391496 | tf_op jit(solution)/shard_map/ppermute | solution.py:31
  69.6 0.0 collective-permute-start.13
  69.6 0.1 pad_maximum_fusion.1.refs_0_
  69.7 0.1 collective-permute-start.14
  69.8 1.5 collective-permute-start.15
  71.3 1.2 collective-permute-start.16
  72.5 2.8 %collective-permute-start.17 = (f32[4,64,8,128]{3,2,1,0:T(8,128)S(1)}, f32[4,64,8,128]{3,2,1,0:T(8,128)S(1)}, u32[]{:S(2)}, u32[]{:S(2)}) collective-permute-start(f32[4,64,8,128]{3,2,1,0:T(8,128)S(1)} %pad_maximum_fusion.1.refs_0_), channel_id=1, source_target_pairs={{0,1},{1,0},{2,3},{3,2},{4,5},{5,4},{6,7},{7,6},{8,9},{9,8},{10,11... | collective-permute-start | bytes 3145736 | tf_op jit(solution)/shard_map/ppermute | solution.py:31
  75.4 0.0 collective-permute-done.13.refs_7_
  75.4 28.6 %forward_first.1 = (f32[80,1024]{1,0:T(8,128)S(1)}, f32[2,1024,8,128]{3,2,1,0:T(8,128)S(1)}, f32[2,1024,8,128]{3,2,1,0:T(8,128)S(1)}, f32[128,1024]{1,0:T(8,128)...) custom-call(f32[1,1024]{1,0:T(1,128)S(1)} %bitcast.78, f32[4,69,8,128]{3,2,1,0:T(8,128)S(1)} %pad_maximum_fusion.refs_0_, ...), custom_call_target="tpu_custom_call" | custom-call | tf_op jit(solution)/shard_map/forward_first/pallas_call | solution.py:322
  104.0 0.0 collective-permute-done.15.refs_2_
  104.0 0.0 collective-permute-done.16.refs_3_
  104.0 0.1 collective-permute-start.18
  104.1 0.5 collective-permute-start.19
  104.6 0.1 collective-permute-start.20
  104.7 16.6 %forward_second.1 = (f32[8,128]{1,0:T(8,128)}, f32[128,1024]{1,0:T(8,128)S(1)}, f32[128,1024]{1,0:T(8,128)S(1)}) custom-call(f32[16,128]{1,0:T(8,128)S(1)} %get-tuple-element.15.seen, f32[80,1024]{1,0:T(8,128)S(1)} %get-tuple-element.17.earlier, f32[2,1024,8,128]{3,2,1,0:T(8,128)S(1)} %get-tuple-element.18.mats, ...), custom_call_target="tpu_custom_call" | custom-call | tf_op jit(solution)/shard_map/forward_second/pallas_call | solution.py:342
  121.3 0.0 collective-permute-done.17.refs_4_
  121.3 0.0 collective-permute-done.19.refs_6_
  121.4 0.0 collective-permute-done.20.refs_7_
  121.4 41.5 %backward_chain.1 = f32[8,128]{1,0:T(8,128)} custom-call(f32[16,128]{1,0:T(8,128)S(1)} %get-tuple-element.15.seen, f32[128,1024]{1,0:T(8,128)S(1)} %get-tuple-element.23.error, f32[128,1024]{1,0:T(8,128)S(1)} %get-tuple-element.24.prior, f32[4,64,8,128]{3,2,1,0:T(8,128)S(1)} %pad_maximum_fusion.1.refs_0_, ...), custom_call_target="tpu_custom_call" | custom-call | tf_op jit(solution)/shard_map/backward_chain/pallas_call | solution.py:352
  (30 shorter events, 0.3 us)
Async XLA Ops:
  0.6 3.0 %copy-start = (f32[8,1024]{1,0:T(8,128)S(1)}, f32[8,1024]{1,0:T(8,128)}, u32[]{:S(2)}) copy-start(f32[8,1024]{1,0:T(8,128)} %param.8) | copy-start | bytes 98308
  1.5 5.6 %collective-permute-start = (f32[2,8,8,128]{3,2,1,0:T(8,128)S(1)}, f32[2,8,8,128]{3,2,1,0:T(8,128)S(1)}, u32[]{:S(2)}, u32[]{:S(2)}) collective-permute-start(f32[2,8,8,128]{3,2,1,0:T(8,128)S(1)} %get-tuple-element.37), channel_id=1, source_target_pairs={{0,1},{1,0},{2,3},{3,2},{4,5},{5,4},{6,7},{7,6},{8,9},{9,8},{10,11... | collective-permute-start | bytes 196616 | tf_op jit(solution)/shard_map/ppermute | solution.py:31
  7.1 7.8 %collective-permute-start.1 = (f32[2,16,8,128]{3,2,1,0:T(8,128)S(1)}, f32[2,16,8,128]{3,2,1,0:T(8,128)S(1)}, u32[]{:S(2)}, u32[]{:S(2)}) collective-permute-start(f32[2,16,8,128]{3,2,1,0:T(8,128)S(1)} %maximum_select_fusion), channel_id=1, source_target_pairs={{0,2},{1,3},{2,4},{3,5},{4,6},{5,7},{6,0},{7,1},{8,10},{9,11},{10,... | collective-permute-start | bytes 393224 | tf_op jit(solution)/shard_map/ppermute | solution.py:35
  8.9 9.7 %collective-permute-start.2 = (f32[2,16,8,128]{3,2,1,0:T(8,128)S(1)}, f32[2,16,8,128]{3,2,1,0:T(8,128)S(1)}, u32[]{:S(2)}, u32[]{:S(2)}) collective-permute-start(f32[2,16,8,128]{3,2,1,0:T(8,128)S(1)} %maximum_select_fusion), channel_id=1, source_target_pairs={{0,4},{1,5},{2,6},{3,7},{4,0},{5,1},{6,2},{7,3},{8,12},{9,13},{10,... | collective-permute-start | bytes 393224 | tf_op jit(solution)/shard_map/ppermute | solution.py:35
  12.2 6.4 %collective-permute-start.3 = (f32[2,16,8,128]{3,2,1,0:T(8,128)S(1)}, f32[2,16,8,128]{3,2,1,0:T(8,128)S(1)}, u32[]{:S(2)}, u32[]{:S(2)}) collective-permute-start(f32[2,16,8,128]{3,2,1,0:T(8,128)S(1)} %maximum_select_fusion), channel_id=1, source_target_pairs={{0,6},{1,7},{2,0},{3,1},{4,2},{5,3},{6,4},{7,5},{8,14},{9,15},{10,... | collective-permute-start | bytes 393224 | tf_op jit(solution)/shard_map/ppermute | solution.py:35
  18.8 15.0 %collective-permute-start.6 = (f32[133,8,128]{2,1,0:T(8,128)S(1)}, f32[133,8,128]{2,1,0:T(8,128)S(1)}, u32[]{:S(2)}, u32[]{:S(2)}) collective-permute-start(f32[133,8,128]{2,1,0:T(8,128)S(1)} %get-tuple-element.29), channel_id=1, source_target_pairs={{0,24},{1,97},{2,26},{3,99},{4,28},{5,101},{6,30},{7,103},{8,0},{9... | collective-permute-start | bytes 1634312 | tf_op jit(solution)/shard_map/ppermute | solution.py:44
  21.6 12.2 %collective-permute-start.5 = (f32[133,8,128]{2,1,0:T(8,128)S(1)}, f32[133,8,128]{2,1,0:T(8,128)S(1)}, u32[]{:S(2)}, u32[]{:S(2)}) collective-permute-start(f32[133,8,128]{2,1,0:T(8,128)S(1)} %get-tuple-element.29), channel_id=1, source_target_pairs={{0,16},{1,65},{2,18},{3,67},{4,20},{5,69},{6,22},{7,71},{8,24},{9,... | collective-permute-start | bytes 1634312 | tf_op jit(solution)/shard_map/ppermute | solution.py:44
  21.9 15.5 %collective-permute-start.4 = (f32[133,8,128]{2,1,0:T(8,128)S(1)}, f32[133,8,128]{2,1,0:T(8,128)S(1)}, u32[]{:S(2)}, u32[]{:S(2)}) collective-permute-start(f32[133,8,128]{2,1,0:T(8,128)S(1)} %get-tuple-element.29), channel_id=1, source_target_pairs={{0,8},{1,33},{2,10},{3,35},{4,12},{5,37},{6,14},{7,39},{8,16},{9,4... | collective-permute-start | bytes 1634312 | tf_op jit(solution)/shard_map/ppermute | solution.py:44
  37.5 16.1 %collective-permute-start.7 = (f32[4,69,8,128]{3,2,1,0:T(8,128)S(1)}, f32[4,69,8,128]{3,2,1,0:T(8,128)S(1)}, u32[]{:S(2)}, u32[]{:S(2)}) collective-permute-start(f32[4,69,8,128]{3,2,1,0:T(8,128)S(1)} %pad_maximum_fusion.refs_0_), channel_id=1, source_target_pairs={{0,32},{1,9},{2,34},{3,11},{4,36},{5,13},{6,38},{7,15},{8,40},{9,1... | collective-permute-start | bytes 3391496 | tf_op jit(solution)/shard_map/ppermute | solution.py:44
  38.5 27.9 %collective-permute-start.8 = (f32[4,69,8,128]{3,2,1,0:T(8,128)S(1)}, f32[4,69,8,128]{3,2,1,0:T(8,128)S(1)}, u32[]{:S(2)}, u32[]{:S(2)}) collective-permute-start(f32[4,69,8,128]{3,2,1,0:T(8,128)S(1)} %pad_maximum_fusion.refs_0_), channel_id=1, source_target_pairs={{0,64},{1,17},{2,66},{3,19},{4,68},{5,21},{6,70},{7,23},{8,72},{9,... | collective-permute-start | bytes 3391496 | tf_op jit(solution)/shard_map/ppermute | solution.py:44
  41.1 28.5 %collective-permute-start.9 = (f32[4,69,8,128]{3,2,1,0:T(8,128)S(1)}, f32[4,69,8,128]{3,2,1,0:T(8,128)S(1)}, u32[]{:S(2)}, u32[]{:S(2)}) collective-permute-start(f32[4,69,8,128]{3,2,1,0:T(8,128)S(1)} %pad_maximum_fusion.refs_0_), channel_id=1, source_target_pairs={{0,96},{1,25},{2,98},{3,27},{4,100},{5,29},{6,102},{7,31},{8,104},... | collective-permute-start | bytes 3391496 | tf_op jit(solution)/shard_map/ppermute | solution.py:44
  42.2 27.5 %collective-permute-start.10 = (f32[4,69,8,128]{3,2,1,0:T(8,128)S(1)}, f32[4,69,8,128]{3,2,1,0:T(8,128)S(1)}, u32[]{:S(2)}, u32[]{:S(2)}) collective-permute-start(f32[4,69,8,128]{3,2,1,0:T(8,128)S(1)} %pad_maximum_fusion.refs_0_), channel_id=1, source_target_pairs={{0,1},{1,0},{2,3},{3,2},{4,5},{5,4},{6,7},{7,6},{8,9},{9,8},{10,11... | collective-permute-start | bytes 3391496 | tf_op jit(solution)/shard_map/ppermute | solution.py:31
  53.7 17.6 %collective-permute-start.11 = (f32[4,69,8,128]{3,2,1,0:T(8,128)S(1)}, f32[4,69,8,128]{3,2,1,0:T(8,128)S(1)}, u32[]{:S(2)}, u32[]{:S(2)}) collective-permute-start(f32[4,69,8,128]{3,2,1,0:T(8,128)S(1)} %collective-permute-done.7.refs_1_), channel_id=1, source_target_pairs={{0,1},{1,0},{2,3},{3,2},{4,5},{5,4},{6,7},{7,6},{8,9},{9,8},{10,11... | collective-permute-start | bytes 3391496 | tf_op jit(solution)/shard_map/ppermute | solution.py:31
  56.4 19.0 %copy-start.1 = (f32[1024]{0:T(1024)S(1)}, f32[1024]{0:T(1024)}, u32[]{:S(2)}) copy-start(f32[1024]{0:T(1024)} %param.10) | copy-start | bytes 12292
  66.5 6.1 %collective-permute-start.12 = (f32[4,69,8,128]{3,2,1,0:T(8,128)S(1)}, f32[4,69,8,128]{3,2,1,0:T(8,128)S(1)}, u32[]{:S(2)}, u32[]{:S(2)}) collective-permute-start(f32[4,69,8,128]{3,2,1,0:T(8,128)S(1)} %collective-permute-done.8.refs_2_), channel_id=1, source_target_pairs={{0,1},{1,0},{2,3},{3,2},{4,5},{5,4},{6,7},{7,6},{8,9},{9,8},{10,11... | collective-permute-start | bytes 3391496 | tf_op jit(solution)/shard_map/ppermute | solution.py:31
  69.6 5.7 %collective-permute-start.13 = (f32[4,69,8,128]{3,2,1,0:T(8,128)S(1)}, f32[4,69,8,128]{3,2,1,0:T(8,128)S(1)}, u32[]{:S(2)}, u32[]{:S(2)}) collective-permute-start(f32[4,69,8,128]{3,2,1,0:T(8,128)S(1)} %collective-permute-done.9.refs_3_), channel_id=1, source_target_pairs={{0,1},{1,0},{2,3},{3,2},{4,5},{5,4},{6,7},{7,6},{8,9},{9,8},{10,11... | collective-permute-start | bytes 3391496 | tf_op jit(solution)/shard_map/ppermute | solution.py:31
  69.7 34.3 %collective-permute-start.14 = (f32[4,64,8,128]{3,2,1,0:T(8,128)S(1)}, f32[4,64,8,128]{3,2,1,0:T(8,128)S(1)}, u32[]{:S(2)}, u32[]{:S(2)}) collective-permute-start(f32[4,64,8,128]{3,2,1,0:T(8,128)S(1)} %pad_maximum_fusion.1.refs_0_), channel_id=1, source_target_pairs={{0,32},{1,9},{2,34},{3,11},{4,36},{5,13},{6,38},{7,15},{8,40},{9,1... | collective-permute-start | bytes 3145736 | tf_op jit(solution)/shard_map/ppermute | solution.py:44
  69.8 34.2 %collective-permute-start.15 = (f32[4,64,8,128]{3,2,1,0:T(8,128)S(1)}, f32[4,64,8,128]{3,2,1,0:T(8,128)S(1)}, u32[]{:S(2)}, u32[]{:S(2)}) collective-permute-start(f32[4,64,8,128]{3,2,1,0:T(8,128)S(1)} %pad_maximum_fusion.1.refs_0_), channel_id=1, source_target_pairs={{0,64},{1,17},{2,66},{3,19},{4,68},{5,21},{6,70},{7,23},{8,72},{9,... | collective-permute-start | bytes 3145736 | tf_op jit(solution)/shard_map/ppermute | solution.py:44
  71.3 32.7 %collective-permute-start.16 = (f32[4,64,8,128]{3,2,1,0:T(8,128)S(1)}, f32[4,64,8,128]{3,2,1,0:T(8,128)S(1)}, u32[]{:S(2)}, u32[]{:S(2)}) collective-permute-start(f32[4,64,8,128]{3,2,1,0:T(8,128)S(1)} %pad_maximum_fusion.1.refs_0_), channel_id=1, source_target_pairs={{0,96},{1,25},{2,98},{3,27},{4,100},{5,29},{6,102},{7,31},{8,104},... | collective-permute-start | bytes 3145736 | tf_op jit(solution)/shard_map/ppermute | solution.py:44
  72.5 48.8 %collective-permute-start.17 = (f32[4,64,8,128]{3,2,1,0:T(8,128)S(1)}, f32[4,64,8,128]{3,2,1,0:T(8,128)S(1)}, u32[]{:S(2)}, u32[]{:S(2)}) collective-permute-start(f32[4,64,8,128]{3,2,1,0:T(8,128)S(1)} %pad_maximum_fusion.1.refs_0_), channel_id=1, source_target_pairs={{0,1},{1,0},{2,3},{3,2},{4,5},{5,4},{6,7},{7,6},{8,9},{9,8},{10,11... | collective-permute-start | bytes 3145736 | tf_op jit(solution)/shard_map/ppermute | solution.py:31
  104.0 17.3 %collective-permute-start.18 = (f32[4,64,8,128]{3,2,1,0:T(8,128)S(1)}, f32[4,64,8,128]{3,2,1,0:T(8,128)S(1)}, u32[]{:S(2)}, u32[]{:S(2)}) collective-permute-start(f32[4,64,8,128]{3,2,1,0:T(8,128)S(1)} %collective-permute-done.14.refs_1_), channel_id=1, source_target_pairs={{0,1},{1,0},{2,3},{3,2},{4,5},{5,4},{6,7},{7,6},{8,9},{9,8},{10,11... | collective-permute-start | bytes 3145736 | tf_op jit(solution)/shard_map/ppermute | solution.py:31
  104.1 17.2 %collective-permute-start.19 = (f32[4,64,8,128]{3,2,1,0:T(8,128)S(1)}, f32[4,64,8,128]{3,2,1,0:T(8,128)S(1)}, u32[]{:S(2)}, u32[]{:S(2)}) collective-permute-start(f32[4,64,8,128]{3,2,1,0:T(8,128)S(1)} %collective-permute-done.15.refs_2_), channel_id=1, source_target_pairs={{0,1},{1,0},{2,3},{3,2},{4,5},{5,4},{6,7},{7,6},{8,9},{9,8},{10,11... | collective-permute-start | bytes 3145736 | tf_op jit(solution)/shard_map/ppermute | solution.py:31
  104.6 16.7 %collective-permute-start.20 = (f32[4,64,8,128]{3,2,1,0:T(8,128)S(1)}, f32[4,64,8,128]{3,2,1,0:T(8,128)S(1)}, u32[]{:S(2)}, u32[]{:S(2)}) collective-permute-start(f32[4,64,8,128]{3,2,1,0:T(8,128)S(1)} %collective-permute-done.16.refs_3_), channel_id=1, source_target_pairs={{0,1},{1,0},{2,3},{3,2},{4,5},{5,4},{6,7},{7,6},{8,9},{9,8},{10,11... | collective-permute-start | bytes 3145736 | tf_op jit(solution)/shard_map/ppermute | solution.py:31
